TPU v7x, 128 devices: a whole 4x4x4 slice. The times are simulated.
128 devices in a mesh: bricks: 32 (over z, y, core), slab: 4 (over x).
Axes of the slice: x: 4, y: 4, z: 4, core: 2. Of those that a mesh axis runs over, the one named last changes fastest.
Arguments:
- observed: float32 [32, 64, 16, 128], P('bricks', 'slab'), may hold values from -6 to 6
- estimate: float32 [32, 64, 16, 128], P('bricks', 'slab'), may hold values from -6 to 6
- blur_taps: float32 [3, 15], replicated, may hold values from 0.02 to 0.15
- slot_brick: int32 [32], replicated, may hold values from 0 to 31, as said below
- neighbours: int32 [32, 6], replicated, may hold values from -1 to 31, as said below
- coords: int32 [32, 3], replicated, may hold values from 0 to 3, as said below
Outputs:
- solution: float32 [32, 64, 16, 128], P('bricks', 'slab')
- residual: float32 [32, 64, 16, 128], P('bricks', 'slab')
Inputs may be any that keep to these rules, and one draw needn't show every extreme that they name: `slot_brick`: each brick number appears in exactly one row. neighbours[i, k] is the brick whose coords differ from brick i's by one along face k (order -z, +z, -y, +y, -x, +x), or -1 where no active brick sits there. `coords`: distinct positions, column 0 below 4, column 1 below 4, column 2 below 4.
All inputs are finite; a program needn't handle non-finite values.
Results may differ from a plain program's by a relative error of at most 0.0003.
Values sent between devices are 32-bit elements; how exact they have to be, the bound alone decides.
A program may use at most 64 MiB of HBM per device.

v0:
```python
import jax
import jax.numpy as jnp
from jax import lax
from jax.sharding import PartitionSpec as P

BZ = 64
CG_STEPS = 2
GZ = 4


SHRINK = 0.5
WEIGHT = 0.3


def padded_2(cells, sides, width):
    for axis, dim in sides:
        count = lax.axis_size(axis)
        head = lax.slice_in_dim(cells, 0, width, axis=dim)
        tail = lax.slice_in_dim(cells, cells.shape[dim] - width, cells.shape[dim], axis=dim)
        cells = jnp.concatenate(
            [
                lax.ppermute(tail, axis, [(i, (i + 1) % count) for i in range(count)]),
                cells,
                lax.ppermute(head, axis, [((i + 1) % count, i) for i in range(count)]),
            ],
            axis=dim,
        )
    return cells


def take_face(volume, dimension, start, halo_width):
    sliced = lax.slice_in_dim(volume, start, start + halo_width, axis=dimension)
    return jnp.moveaxis(sliced, dimension, 0).reshape(halo_width, -1)


def put_face(flat_face, dimension, full_shape, halo_width):
    reordered = [halo_width] + [
        full_shape[other] for other in range(len(full_shape)) if other != dimension
    ]
    return jnp.moveaxis(flat_face.reshape(reordered), 0, dimension)


def swap_faces(bottom, top_face, lower_row, upper_row):
    peer_ids = jnp.arange(lax.axis_size("bricks"), dtype=jnp.int32)[:, None, None]
    outgoing = jnp.where(peer_ids == upper_row, top_face[None], 0.0) + jnp.where(
        peer_ids == lower_row, bottom[None], 0.0
    )
    incoming = lax.all_to_all(outgoing, "bricks", split_axis=0, concat_axis=0, tiled=True)
    under_halo = jnp.sum(jnp.where(peer_ids == lower_row, incoming, 0.0), axis=0)
    over_halo = jnp.sum(jnp.where(peer_ids == upper_row, incoming, 0.0), axis=0)
    return (under_halo, over_halo)


def side_halo(volume, dimension, reach, peer_rows):
    extent = volume.shape[dimension]
    bottom = take_face(volume, dimension, 0, reach)
    top_face = take_face(volume, dimension, extent - reach, reach)
    under_halo, over_halo = swap_faces(
        bottom, top_face, peer_rows[2 * dimension], peer_rows[2 * dimension + 1]
    )
    return (
        put_face(under_halo, dimension, volume.shape, reach),
        put_face(over_halo, dimension, volume.shape, reach),
    )


def depth_halo(volume, reach, context):
    peer_rows, slab_pos, slab_count = (context[0], context[1], context[2])
    extent = volume.shape[0]
    bottom = take_face(volume, 0, 0, reach)
    top_face = take_face(volume, 0, extent - reach, reach)
    from_under, from_over = swap_faces(bottom, top_face, peer_rows[0], peer_rows[1])
    to_lower = jnp.where(slab_pos == 0, from_over, bottom)
    to_upper = jnp.where(slab_pos == slab_count - 1, from_under, top_face)
    nearby = padded_2(jnp.concatenate([to_lower, to_upper], 0), (("slab", 0),), reach)
    under_halo = nearby[:reach]
    over_halo = nearby[3 * reach :]
    return (
        put_face(under_halo, 0, volume.shape, reach),
        put_face(over_halo, 0, volume.shape, reach),
    )


def edge_halo(volume, peer_rows):
    peer_ids = jnp.arange(lax.axis_size("bricks"), dtype=jnp.int32)[:, None, None]
    outgoing = []
    for dimension in (1, 2):
        extent = volume.shape[dimension]
        bottom = take_face(volume, dimension, 0, 1)
        top_face = take_face(volume, dimension, extent - 1, 1)
        outgoing.append(
            jnp.where(peer_ids == peer_rows[2 * dimension + 1], top_face[None], 0.0)
            + jnp.where(peer_ids == peer_rows[2 * dimension], bottom[None], 0.0)
        )
    got_y, got_x = (
        lax.all_to_all(outgoing[0], "bricks", split_axis=0, concat_axis=0, tiled=True),
        lax.all_to_all(outgoing[1], "bricks", split_axis=0, concat_axis=0, tiled=True),
    )
    results = []
    for dimension, incoming in ((1, got_y), (2, got_x)):
        under_halo = jnp.sum(jnp.where(peer_ids == peer_rows[2 * dimension], incoming, 0.0), axis=0)
        over_halo = jnp.sum(
            jnp.where(peer_ids == peer_rows[2 * dimension + 1], incoming, 0.0), axis=0
        )
        results.append(put_face(under_halo, dimension, volume.shape, 1))
        results.append(put_face(over_halo, dimension, volume.shape, 1))
    return results


def convolve(padded, kernel, dimension, extent, flipped):
    length = kernel.shape[0]
    summed = None
    for offset in range(length):
        weight = kernel[length - 1 - offset] if flipped else kernel[offset]
        shifted = weight * lax.slice_in_dim(padded, offset, offset + extent, axis=dimension)
        summed = shifted if summed is None else summed + shifted
    return summed


def shrink_gap(values):
    return -SHRINK * values / (values * values + SHRINK)


def identity_map(values):
    return values


def smooth(volume, lows, highs, lower_flags, penalty):
    summed = None
    for dimension in range(3):
        extent = volume.shape[dimension]
        before = jnp.concatenate(
            [lows[dimension], lax.slice_in_dim(volume, 0, extent - 1, axis=dimension)],
            axis=dimension,
        )
        beyond = jnp.concatenate(
            [lax.slice_in_dim(volume, 1, extent, axis=dimension), highs[dimension]], axis=dimension
        )
        position = lax.broadcasted_iota(jnp.int32, volume.shape, dimension)
        keep_low = jnp.where(position == 0, lower_flags[dimension], 1.0)
        part_sum = penalty(volume - before) * keep_low - penalty(beyond - volume)
        summed = part_sum if summed is None else summed + part_sum
    return summed


def operate(volume, context, source):
    peer_rows, lower_flags, damping, blur_taps = (context[0], context[3], context[4], context[5])
    reach = blur_taps.shape[1] // 2
    under_z, over_z = depth_halo(volume, reach, context)
    edges = edge_halo(volume, peer_rows)
    blurred = convolve(
        jnp.concatenate([under_z, volume, over_z], 0), blur_taps[0], 0, volume.shape[0], False
    )
    for dimension in (1, 2):
        under_halo, over_halo = side_halo(blurred, dimension, reach, peer_rows)
        blurred = convolve(
            jnp.concatenate([under_halo, blurred, over_halo], dimension),
            blur_taps[dimension],
            dimension,
            volume.shape[dimension],
            False,
        )
    weighted = damping * damping * blurred
    if source is None:
        flow = weighted
        penalty = identity_map
    else:
        flow = source - weighted
        penalty = shrink_gap
    for dimension in (2, 1):
        under_halo, over_halo = side_halo(flow, dimension, reach, peer_rows)
        flow = convolve(
            jnp.concatenate([under_halo, flow, over_halo], dimension),
            blur_taps[dimension],
            dimension,
            volume.shape[dimension],
            True,
        )
    under_halo, over_halo = depth_halo(flow, reach, context)
    flow = convolve(
        jnp.concatenate([under_halo, flow, over_halo], 0), blur_taps[0], 0, volume.shape[0], True
    )
    lows = (under_z[-1:], edges[0], edges[2])
    highs = (over_z[:1], edges[1], edges[3])
    return flow + WEIGHT * smooth(volume, lows, highs, lower_flags, penalty)


def global_squares(values):
    return lax.psum(jnp.sum(values * values), ("bricks", "slab"))


def shards(observed, estimate, blur_taps, slot_brick, neighbours, coords):
    peer_count = lax.axis_size("bricks")
    my_row = lax.axis_index("bricks")
    slab_pos = lax.axis_index("slab")
    slab_count = lax.axis_size("slab")
    brick_ids = jnp.arange(peer_count, dtype=jnp.int32)
    my_brick = jnp.sum(jnp.where(brick_ids == my_row, slot_brick, 0))
    row_of = jnp.sum(
        jnp.where(slot_brick[None, :] == brick_ids[:, None], brick_ids[None, :], 0), axis=1
    )
    my_links = jnp.sum(jnp.where((brick_ids == my_brick)[:, None], neighbours, 0), axis=0)
    peer_rows = jnp.where(
        my_links >= 0,
        jnp.sum(jnp.where(brick_ids[None, :] == my_links[:, None], row_of[None, :], 0), axis=1),
        -1,
    )
    has_peer = (peer_rows >= 0).astype(jnp.float32)
    lower_flags = (jnp.where(slab_pos > 0, 1.0, has_peer[0]), has_peer[2], has_peer[4])
    volume = estimate[0]
    measured = observed[0]
    depth_count = volume.shape[0]
    layer_z = jnp.sum(jnp.where(brick_ids == my_brick, coords[:, 0], 0))
    depth_cells = layer_z * BZ + slab_pos * depth_count + jnp.arange(depth_count, dtype=jnp.int32)
    damping = jnp.exp(-depth_cells.astype(jnp.float32) / (BZ * GZ))[:, None, None]
    context = (peer_rows, slab_pos, slab_count, lower_flags, damping, blur_taps)
    residual = operate(volume, context, damping * measured)
    direction = residual
    solution = volume
    norm_now = global_squares(residual)
    for cg_step in range(CG_STEPS):
        applied = operate(direction, context, None)
        step_len = norm_now / lax.psum(jnp.sum(direction * applied), ("bricks", "slab"))
        solution = solution + step_len * direction
        residual = residual - step_len * applied
        if cg_step + 1 < CG_STEPS:
            norm_next = global_squares(residual)
            direction = residual + norm_next / norm_now * direction
            norm_now = norm_next
    return (solution[None], residual[None])


def solution(mesh):
    placed = (P("bricks", "slab", None, None), P("bricks", "slab", None, None), P(), P(), P(), P())
    return jax.shard_map(
        shards,
        mesh=mesh,
        in_specs=placed,
        out_specs=(P("bricks", "slab", None, None), P("bricks", "slab", None, None)),
        check_vma=False,
    )
```

profile of v0, /device:TPU:1, one launch (start us, length us, event | category | flops | bytes accessed | tf_op | source)
XLA Modules:
  0.0 980.4 jit_solution(11359285699132627254)
XLA Ops:
  8.9 9.7 all-to-all-start
  20.0 27.2 %all-to-all-done = f32[32,7,2048]{2,1,0:T(8,128)S(1)} async-done(((f32[32,7,2048]{2,1,0:T(8,128)}), f32[32,7,2048]{2,1,0:T(8,128)S(1)}, u32[]{:S(2)}, u32[]{:S(2)}) %all-to-all-start) | async-done | bytes 1835040 | tf_op jit(solution)/shard_map/all_to_all | solution.py:48
  52.8 9.4 fusion.205
  63.9 6.5 all-to-all-start.1
  72.4 26.3 %all-to-all-done.1 = f32[32,7,2048]{2,1,0:T(8,128)S(1)} async-done(((f32[32,7,2048]{2,1,0:T(8,128)}), f32[32,7,2048]{2,1,0:T(8,128)S(1)}, u32[]{:S(2)}, u32[]{:S(2)}) %all-to-all-start.1) | async-done | bytes 1835040 | tf_op jit(solution)/shard_map/all_to_all | solution.py:48
  99.2 9.7 fusion.433
  110.0 5.7 all-to-all-start.2
  118.3 6.3 all-to-all-done.2
  125.1 10.3 %fusion.665 = f32[16,16,128]{2,1,0:T(8,128)S(1)} fusion(f32[16,16,128]{2,1,0:T(8,128)S(1)} %fusion.433, f32[16,16,7]{2,1,0:T(8,128)S(1)} %bitcast.391, f32[16,16,7]{2,1,0:T(8,128)S(1)} %bitcast.390, f32[1,16,16,128]{3,2,1,0:T(8,128)S(1)} %copy-done.10, f32[]{:T(128)} %bitcast.69, f32[]{:T(128)} %bitcast.68, f32[]{:T(128)} %bitcast.67, f32[]{:T(128)} %bitcast.66, ...), kind=kLoop, calls=%fused_computation.1163 | loop fusion | flops 1507328 | bytes 407740 | tf_op jit(solution)/shard_map/sub | solution.py:168
  135.8 12.4 %all_to_all.120 = f32[32,7,256]{2,1,0:T(8,128)S(1)} all-to-all(f32[32,7,256]{2,1,0:T(8,128)S(1)} %select_add_fusion.16), channel_id=1, replica_groups=mesh['bricks'=32,'slab'=4] {'bricks'}, dimensions={0} | all-to-all | bytes 458752 | tf_op jit(solution)/shard_map/all_to_all | solution.py:48
  148.7 10.3 %fusion.625 = f32[16,16,128]{2,1,0:T(8,128)S(1)} fusion(f32[16,16,128]{2,1,0:T(8,128)S(1)} %fusion.665, f32[16,16,7]{2,1,0:T(8,128)S(1)} %bitcast.388, f32[16,16,7]{2,1,0:T(8,128)S(1)} %bitcast.386, f32[]{:T(128)} %bitcast.69, f32[]{:T(128)} %bitcast.68, f32[]{:T(128)} %bitcast.67, f32[]{:T(128)} %bitcast.66, f32[]{:T(128)} %bitcast.65, f32[]{:T(128)} %bitcast.62, ...), kind=kLoop, calls=%fused_computation.1123 | loop fusion | flops 1409024 | bytes 276540 | tf_op jit(solution)/shard_map/add | solution.py:116
  165.6 27.2 %all-to-all-done.4 = f32[32,7,2048]{2,1,0:T(8,128)S(1)} async-done(((f32[32,7,2048]{2,1,0:T(8,128)}), f32[32,7,2048]{2,1,0:T(8,128)S(1)}, u32[]{:S(2)}, u32[]{:S(2)}) %all-to-all-start.4) | async-done | bytes 1835040 | tf_op jit(solution)/shard_map/all_to_all | solution.py:48
  192.7 5.6 all-to-all-start.7
  198.9 9.7 fusion.395
  210.4 8.1 all-to-all-start.5
  224.6 22.4 %all-to-all-done.5 = f32[32,7,2048]{2,1,0:T(8,128)S(1)} async-done(((f32[32,7,2048]{2,1,0:T(8,128)}), f32[32,7,2048]{2,1,0:T(8,128)S(1)}, u32[]{:S(2)}, u32[]{:S(2)}) %all-to-all-start.5) | async-done | bytes 1835040 | tf_op jit(solution)/shard_map/all_to_all | solution.py:48
  255.6 5.6 all-to-all-done.6
  263.4 10.7 %fusion.167 = f32[16,16,128]{2,1,0:T(8,128)S(1)} fusion(f32[16,16,128]{2,1,0:T(8,128)S(1)} %fusion.395, f32[7,16,128]{2,1,0:T(8,128)S(1)} %bitcast.435, f32[7,16,128]{2,1,0:T(8,128)S(1)} %bitcast.433, f32[16,16,1]{2,1,0:T(8,128)S(1)} %transpose_reshape.49, f32[16,16,127]{2,1,0:T(8,128)S(1)} %get-tuple-element.114, ...), kind=kLoop, calls=%fused_computation.665 | loop fusion | flops 2916352 | bytes 1295036 | tf_op jit(solution)/shard_map/add | solution.py:185
  274.5 31.8 %all_to_all.121 = f32[32,7,2048]{2,1,0:T(8,128)S(1)} all-to-all(f32[32,7,2048]{2,1,0:T(8,128)S(1)} %select_add_fusion.7), channel_id=1, replica_groups=mesh['bricks'=32,'slab'=4] {'bricks'}, dimensions={0} | all-to-all | bytes 3670016 | tf_op jit(solution)/shard_map/all_to_all | solution.py:48
  311.9 9.4 fusion.128
  321.7 33.1 %all_to_all.122 = f32[32,7,2048]{2,1,0:T(8,128)S(1)} all-to-all(f32[32,7,2048]{2,1,0:T(8,128)S(1)} %select_add_fusion.6), channel_id=1, replica_groups=mesh['bricks'=32,'slab'=4] {'bricks'}, dimensions={0} | all-to-all | bytes 3670016 | tf_op jit(solution)/shard_map/all_to_all | solution.py:48
  355.3 9.7 fusion.357
  365.4 12.5 %all_to_all.123 = f32[32,7,256]{2,1,0:T(8,128)S(1)} all-to-all(f32[32,7,256]{2,1,0:T(8,128)S(1)} %select_add_fusion.15), channel_id=1, replica_groups=mesh['bricks'=32,'slab'=4] {'bricks'}, dimensions={0} | all-to-all | bytes 458752 | tf_op jit(solution)/shard_map/all_to_all | solution.py:48
  378.3 10.3 %fusion.587 = f32[16,16,128]{2,1,0:T(8,128)S(1)} fusion(f32[16,16,128]{2,1,0:T(8,128)S(1)} %fusion.357, f32[16,16,7]{2,1,0:T(8,128)S(1)} %bitcast.398, f32[16,16,7]{2,1,0:T(8,128)S(1)} %bitcast.393, f32[]{:T(128)} %bitcast.69, f32[]{:T(128)} %bitcast.68, f32[]{:T(128)} %bitcast.67, f32[]{:T(128)} %bitcast.66, f32[]{:T(128)} %bitcast.65, f32[]{:T(128)} %bitcast.62, ...), kind=kLoop, calls=%fused_computation.1085 | loop fusion | flops 1441792 | bytes 276604 | tf_op jit(solution)/shard_map/mul | solution.py:163
  389.0 12.4 %all_to_all.124 = f32[32,7,256]{2,1,0:T(8,128)S(1)} all-to-all(f32[32,7,256]{2,1,0:T(8,128)S(1)} %select_add_fusion.14), channel_id=1, replica_groups=mesh['bricks'=32,'slab'=4] {'bricks'}, dimensions={0} | all-to-all | bytes 458752 | tf_op jit(solution)/shard_map/all_to_all | solution.py:48
  401.9 10.3 %fusion.548 = f32[16,16,128]{2,1,0:T(8,128)S(1)} fusion(f32[16,16,128]{2,1,0:T(8,128)S(1)} %fusion.587, f32[16,16,7]{2,1,0:T(8,128)S(1)} %bitcast.389, f32[16,16,7]{2,1,0:T(8,128)S(1)} %bitcast.387, f32[]{:T(128)} %bitcast.69, f32[]{:T(128)} %bitcast.68, f32[]{:T(128)} %bitcast.67, f32[]{:T(128)} %bitcast.66, f32[]{:T(128)} %bitcast.65, f32[]{:T(128)} %bitcast.62, ...), kind=kLoop, calls=%fused_computation.1046 | loop fusion | flops 1409024 | bytes 276540 | tf_op jit(solution)/shard_map/add | solution.py:116
  419.1 27.3 %all-to-all-done.12 = f32[32,7,2048]{2,1,0:T(8,128)S(1)} async-done(((f32[32,7,2048]{2,1,0:T(8,128)}), f32[32,7,2048]{2,1,0:T(8,128)S(1)}, u32[]{:S(2)}, u32[]{:S(2)}) %all-to-all-start.12) | async-done | bytes 1835040 | tf_op jit(solution)/shard_map/all_to_all | solution.py:48
  452.2 9.7 fusion.319
  464.3 7.5 all-to-all-start.13
  474.2 26.1 %all-to-all-done.13 = f32[32,7,2048]{2,1,0:T(8,128)S(1)} async-done(((f32[32,7,2048]{2,1,0:T(8,128)}), f32[32,7,2048]{2,1,0:T(8,128)S(1)}, u32[]{:S(2)}, u32[]{:S(2)}) %all-to-all-start.13) | async-done | bytes 1835040 | tf_op jit(solution)/shard_map/all_to_all | solution.py:48
  516.9 11.3 %multiply_reduce_fusion.2 = (f32[]{:T(128)}, f32[]{:T(128)}, f32[16,16,128]{2,1,0:T(8,128)S(1)}) fusion(f32[16,16,128]{2,1,0:T(8,128)S(1)} %fusion.167, f32[16,16,1]{2,1,0:T(8,128)S(1)} %transpose_reshape.51, f32[16,16,127]{2,1,0:T(8,128)S(1)} %get-tuple-element.106, f32[128]{0:T(128)} %compare_select_fusion, f32[16,16,127]{2,1,0:T(8,128)S(1)} %get-tuple-element.105, ...), kind=kLoop, calls=%fused_computation.1319 | loop fusion | flops 2260990 | bytes 1295044 | tf_op jit(solution)/shard_map/reduce_sum | solution.py:223
  528.1 64.5 %all-reduce = (f32[]{:T(128)}, f32[]{:T(128)}) all-reduce(f32[]{:T(128)} %get-tuple-element.47, f32[]{:T(128)} %get-tuple-element.46), channel_id=1, replica_groups=mesh['bricks'=32,'slab'=4] {'bricks','slab'}, use_global_device_ids=true, to_apply=%region_22.23 | all-reduce | flops 2 | bytes 16 | tf_op jit(solution)/shard_map/psum | solution.py:189
  594.6 62.8 %psum.30 = f32[]{:T(128)} all-reduce(f32[]{:T(128)} %multiply_reduce_fusion.1), channel_id=1, replica_groups=mesh['bricks'=32,'slab'=4] {'bricks','slab'}, use_global_device_ids=true, to_apply=%region_42.43 | all-reduce | flops 1 | bytes 8 | tf_op jit(solution)/shard_map/psum | solution.py:189
  659.2 33.0 %all_to_all.125 = f32[32,7,2048]{2,1,0:T(8,128)S(1)} all-to-all(f32[32,7,2048]{2,1,0:T(8,128)S(1)} %select_add_fusion.3), channel_id=1, replica_groups=mesh['bricks'=32,'slab'=4] {'bricks'}, dimensions={0} | all-to-all | bytes 3670016 | tf_op jit(solution)/shard_map/all_to_all | solution.py:48
  697.8 9.4 fusion.51
  707.6 33.3 %all_to_all.126 = f32[32,7,2048]{2,1,0:T(8,128)S(1)} all-to-all(f32[32,7,2048]{2,1,0:T(8,128)S(1)} %select_add_fusion.2), channel_id=1, replica_groups=mesh['bricks'=32,'slab'=4] {'bricks'}, dimensions={0} | all-to-all | bytes 3670016 | tf_op jit(solution)/shard_map/all_to_all | solution.py:48
  741.4 9.7 fusion.281
  751.6 12.4 %all_to_all.127 = f32[32,7,256]{2,1,0:T(8,128)S(1)} all-to-all(f32[32,7,256]{2,1,0:T(8,128)S(1)} %select_add_fusion.13), channel_id=1, replica_groups=mesh['bricks'=32,'slab'=4] {'bricks'}, dimensions={0} | all-to-all | bytes 458752 | tf_op jit(solution)/shard_map/all_to_all | solution.py:48
  764.4 10.3 %fusion.510 = f32[16,16,128]{2,1,0:T(8,128)S(1)} fusion(f32[16,16,128]{2,1,0:T(8,128)S(1)} %fusion.281, f32[16,16,7]{2,1,0:T(8,128)S(1)} %bitcast.394, f32[16,16,7]{2,1,0:T(8,128)S(1)} %bitcast.392, f32[]{:T(128)} %bitcast.69, f32[]{:T(128)} %bitcast.68, f32[]{:T(128)} %bitcast.67, f32[]{:T(128)} %bitcast.66, f32[]{:T(128)} %bitcast.65, f32[]{:T(128)} %bitcast.62, ...), kind=kLoop, calls=%fused_computation.1008 | loop fusion | flops 1441792 | bytes 276604 | tf_op jit(solution)/shard_map/mul | solution.py:163
  775.1 12.4 %all_to_all.128 = f32[32,7,256]{2,1,0:T(8,128)S(1)} all-to-all(f32[32,7,256]{2,1,0:T(8,128)S(1)} %select_add_fusion.12), channel_id=1, replica_groups=mesh['bricks'=32,'slab'=4] {'bricks'}, dimensions={0} | all-to-all | bytes 458752 | tf_op jit(solution)/shard_map/all_to_all | solution.py:48
  788.0 10.3 %fusion.471 = f32[16,16,128]{2,1,0:T(8,128)S(1)} fusion(f32[16,16,128]{2,1,0:T(8,128)S(1)} %fusion.510, f32[16,16,7]{2,1,0:T(8,128)S(1)} %bitcast.385, f32[16,16,7]{2,1,0:T(8,128)S(1)} %bitcast.384, f32[]{:T(128)} %bitcast.69, f32[]{:T(128)} %bitcast.68, f32[]{:T(128)} %bitcast.67, f32[]{:T(128)} %bitcast.66, f32[]{:T(128)} %bitcast.65, f32[]{:T(128)} %bitcast.62, ...), kind=kLoop, calls=%fused_computation.969 | loop fusion | flops 1409024 | bytes 276540 | tf_op jit(solution)/shard_map/add | solution.py:116
  804.9 27.1 %all-to-all-done.20 = f32[32,7,2048]{2,1,0:T(8,128)S(1)} async-done(((f32[32,7,2048]{2,1,0:T(8,128)}), f32[32,7,2048]{2,1,0:T(8,128)S(1)}, u32[]{:S(2)}, u32[]{:S(2)}) %all-to-all-start.20) | async-done | bytes 1835040 | tf_op jit(solution)/shard_map/all_to_all | solution.py:48
  832.0 5.6 all-to-all-start.23
  838.2 9.7 fusion.243
  849.6 7.5 all-to-all-start.21
  860.3 25.5 %all-to-all-done.21 = f32[32,7,2048]{2,1,0:T(8,128)S(1)} async-done(((f32[32,7,2048]{2,1,0:T(8,128)}), f32[32,7,2048]{2,1,0:T(8,128)S(1)}, u32[]{:S(2)}, u32[]{:S(2)}) %all-to-all-start.21) | async-done | bytes 1835040 | tf_op jit(solution)/shard_map/all_to_all | solution.py:48
  902.2 11.4 %multiply_reduce_fusion = (f32[]{:T(128)}, f32[16,16,128]{2,1,0:T(8,128)S(1)}) fusion(f32[16,16,128]{2,1,0:T(8,128)S(1)} %multiply_add_fusion, f32[16,16,1]{2,1,0:T(8,128)S(1)} %transpose_reshape.53, f32[16,16,127]{2,1,0:T(8,128)} %get-tuple-element.86, f32[128]{0:T(128)} %compare_select_fusion, f32[16,16,127]{2,1,0:T(8,128)} %get-tuple-element.85, ...), kind=kLoop, calls=%fused_computation.1315 | loop fusion | flops 2195455 | bytes 1295040 | tf_op jit(solution)/shard_map/reduce_sum | solution.py:223
  913.6 64.5 %psum.31 = f32[]{:T(128)} all-reduce(f32[]{:T(128)} %get-tuple-element.60), channel_id=1, replica_groups=mesh['bricks'=32,'slab'=4] {'bricks','slab'}, use_global_device_ids=true, to_apply=%region_60.61 | all-reduce | flops 1 | bytes 8 | tf_op jit(solution)/shard_map/psum | solution.py:223
  (279 shorter events, 128.5 us)
Async XLA Ops:
  7.2 201.5 %copy-start.11 = (pred[32]{0:T(512)(128)(4,1)}, pred[32]{0:T(512)(128)(4,1)S(1)}, u32[]{:S(2)}) copy-start(pred[32]{0:T(512)(128)(4,1)S(1)} %get-tuple-element.183) | copy-start | bytes 100
  7.2 201.5 %copy-start.17 = (pred[32]{0:T(512)(128)(4,1)}, pred[32]{0:T(512)(128)(4,1)S(1)}, u32[]{:S(2)}) copy-start(pred[32]{0:T(512)(128)(4,1)S(1)} %get-tuple-element.184) | copy-start | bytes 100
  8.9 9.8 copy-start.9
  8.9 38.3 %all-to-all-start = ((f32[32,7,2048]{2,1,0:T(8,128)}), f32[32,7,2048]{2,1,0:T(8,128)S(1)}, u32[]{:S(2)}, u32[]{:S(2)}) async-start(f32[32,7,2048]{2,1,0:T(8,128)} %select_add_fusion.11), calls=%async_computation | async-start | bytes 4194304 | tf_op jit(solution)/shard_map/all_to_all | solution.py:48
  18.6 34.1 %copy-start = (f32[1,16,16,128]{3,2,1,0:T(8,128)S(1)}, f32[1,16,16,128]{3,2,1,0:T(8,128)}, u32[]{:S(2)}) copy-start(f32[1,16,16,128]{3,2,1,0:T(8,128)} %param.7) | copy-start | bytes 393220
  47.7 4.4 collective-permute-start
  49.0 3.2 collective-permute-start.1
  52.7 11.1 %copy-start.24 = (f32[7,2048]{1,0:T(8,128)}, f32[7,2048]{1,0:T(8,128)S(1)}, u32[]{:S(2)}) copy-start(f32[7,2048]{1,0:T(8,128)S(1)} %collective-permute-done.1) | copy-start | bytes 172036
  63.9 34.8 %all-to-all-start.1 = ((f32[32,7,2048]{2,1,0:T(8,128)}), f32[32,7,2048]{2,1,0:T(8,128)S(1)}, u32[]{:S(2)}, u32[]{:S(2)}) async-start(f32[32,7,2048]{2,1,0:T(8,128)} %select_add_fusion.10), calls=%async_computation.1 | async-start | bytes 4194304 | tf_op jit(solution)/shard_map/all_to_all | solution.py:48
  72.4 52.7 %copy-start.10 = (f32[1,16,16,128]{3,2,1,0:T(8,128)S(1)}, f32[1,16,16,128]{3,2,1,0:T(8,128)}, u32[]{:S(2)}) copy-start(f32[1,16,16,128]{3,2,1,0:T(8,128)} %param.6) | copy-start | bytes 393220
  110.0 14.7 %all-to-all-start.2 = ((f32[32,7,256]{2,1,0:T(8,128)}), f32[32,7,256]{2,1,0:T(8,128)S(1)}, u32[]{:S(2)}, u32[]{:S(2)}) async-start(f32[32,7,256]{2,1,0:T(8,128)} %select_add_fusion.17), calls=%async_computation.2 | async-start | bytes 524288 | tf_op jit(solution)/shard_map/all_to_all | solution.py:48
  118.3 40.6 %copy-start.29 = (f32[16]{0:T(128)}, f32[16]{0:T(128)S(1)}, u32[]{:S(2)}) copy-start(f32[16]{0:T(128)S(1)} %get-tuple-element.190) | copy-start | bytes 196
  160.6 32.1 %all-to-all-start.4 = ((f32[32,7,2048]{2,1,0:T(8,128)}), f32[32,7,2048]{2,1,0:T(8,128)S(1)}, u32[]{:S(2)}, u32[]{:S(2)}) async-start(f32[32,7,2048]{2,1,0:T(8,128)} %select_add_fusion.9), calls=%async_computation.4 | async-start | bytes 4194304 | tf_op jit(solution)/shard_map/all_to_all | solution.py:48
  192.7 17.6 %all-to-all-start.7 = ((f32[32,1,256]{2,1,0:T(1,128)}), f32[32,1,256]{2,1,0:T(1,128)S(1)}, u32[]{:S(2)}, u32[]{:S(2)}) async-start(f32[32,1,256]{2,1,0:T(1,128)} %fusion.754), calls=%async_computation.7 | async-start | bytes 65536 | tf_op jit(solution)/shard_map/all_to_all | solution.py:97
  210.4 36.6 %all-to-all-start.5 = ((f32[32,7,2048]{2,1,0:T(8,128)}), f32[32,7,2048]{2,1,0:T(8,128)S(1)}, u32[]{:S(2)}, u32[]{:S(2)}) async-start(f32[32,7,2048]{2,1,0:T(8,128)} %select_add_fusion.8), calls=%async_computation.5 | async-start | bytes 4194304 | tf_op jit(solution)/shard_map/all_to_all | solution.py:48
  218.4 33.7 %copy-start.12 = (pred[32]{0:T(512)(128)(4,1)S(1)}, pred[32]{0:T(512)(128)(4,1)}, u32[]{:S(2)}) copy-start(pred[32]{0:T(512)(128)(4,1)} %copy-done.11) | copy-start | bytes 100
  218.5 33.7 %copy-start.18 = (pred[32]{0:T(512)(128)(4,1)S(1)}, pred[32]{0:T(512)(128)(4,1)}, u32[]{:S(2)}) copy-start(pred[32]{0:T(512)(128)(4,1)} %copy-done.17) | copy-start | bytes 100
  247.0 14.2 %all-to-all-start.6 = ((f32[32,1,2048]{2,1,0:T(1,128)}), f32[32,1,2048]{2,1,0:T(1,128)S(1)}, u32[]{:S(2)}, u32[]{:S(2)}) async-start(f32[32,1,2048]{2,1,0:T(1,128)} %fusion), calls=%async_computation.6 | async-start | bytes 524288 | tf_op jit(solution)/shard_map/all_to_all | solution.py:96
  252.7 21.5 %copy-start.13 = (pred[32]{0:T(512)(128)(4,1)S(1)}, pred[32]{0:T(512)(128)(4,1)}, u32[]{:S(2)}) copy-start(pred[32]{0:T(512)(128)(4,1)} %copy-done.11) | copy-start | bytes 100
  252.7 21.5 %copy-start.19 = (pred[32]{0:T(512)(128)(4,1)S(1)}, pred[32]{0:T(512)(128)(4,1)}, u32[]{:S(2)}) copy-start(pred[32]{0:T(512)(128)(4,1)} %copy-done.17) | copy-start | bytes 100
  252.7 10.6 %collective-permute-start.2 = (f32[7,2048]{1,0:T(8,128)S(1)}, f32[7,2048]{1,0:T(8,128)S(1)}, u32[]{:S(2)}, u32[]{:S(2)}) collective-permute-start(f32[7,2048]{1,0:T(8,128)S(1)} %broadcast_select_fusion.34), channel_id=1, source_target_pairs={{0,1},{1,2},{2,3},{3,0},{4,5},{5,6},{6,7},{7,4},{8,9},{9,10},{10,1... | collective-permute-start | bytes 172040 | tf_op jit(solution)/shard_map/ppermute | solution.py:22
  253.8 9.6 collective-permute-start.3
  306.9 4.4 collective-permute-start.4
  307.9 3.3 collective-permute-start.5
  311.3 10.1 %copy-start.27 = (f32[7,2048]{1,0:T(8,128)}, f32[7,2048]{1,0:T(8,128)S(1)}, u32[]{:S(2)}) copy-start(f32[7,2048]{1,0:T(8,128)S(1)} %collective-permute-done.4) | copy-start | bytes 172036
  354.8 23.6 %copy-start.30 = (f32[16]{0:T(128)S(1)}, f32[16]{0:T(128)}, u32[]{:S(2)}) copy-start(f32[16]{0:T(128)} %copy-done.29) | copy-start | bytes 196
  413.8 32.6 %all-to-all-start.12 = ((f32[32,7,2048]{2,1,0:T(8,128)}), f32[32,7,2048]{2,1,0:T(8,128)S(1)}, u32[]{:S(2)}, u32[]{:S(2)}) async-start(f32[32,7,2048]{2,1,0:T(8,128)} %select_add_fusion.5), calls=%async_computation.12 | async-start | bytes 4194304 | tf_op jit(solution)/shard_map/all_to_all | solution.py:48
  417.9 44.7 %copy-start.14 = (pred[32]{0:T(512)(128)(4,1)S(1)}, pred[32]{0:T(512)(128)(4,1)}, u32[]{:S(2)}) copy-start(pred[32]{0:T(512)(128)(4,1)} %copy-done.11) | copy-start | bytes 100
  417.9 44.7 %copy-start.20 = (pred[32]{0:T(512)(128)(4,1)S(1)}, pred[32]{0:T(512)(128)(4,1)}, u32[]{:S(2)}) copy-start(pred[32]{0:T(512)(128)(4,1)} %copy-done.17) | copy-start | bytes 100
  446.4 17.8 %all-to-all-start.15 = ((f32[32,1,256]{2,1,0:T(1,128)}), f32[32,1,256]{2,1,0:T(1,128)S(1)}, u32[]{:S(2)}, u32[]{:S(2)}) async-start(f32[32,1,256]{2,1,0:T(1,128)} %fusion.755), calls=%async_computation.15 | async-start | bytes 65536 | tf_op jit(solution)/shard_map/all_to_all | solution.py:97
  464.3 36.1 %all-to-all-start.13 = ((f32[32,7,2048]{2,1,0:T(8,128)}), f32[32,7,2048]{2,1,0:T(8,128)S(1)}, u32[]{:S(2)}, u32[]{:S(2)}) async-start(f32[32,7,2048]{2,1,0:T(8,128)} %select_add_fusion.4), calls=%async_computation.13 | async-start | bytes 4194304 | tf_op jit(solution)/shard_map/all_to_all | solution.py:48
  500.4 14.2 %all-to-all-start.14 = ((f32[32,1,2048]{2,1,0:T(1,128)}), f32[32,1,2048]{2,1,0:T(1,128)S(1)}, u32[]{:S(2)}, u32[]{:S(2)}) async-start(f32[32,1,2048]{2,1,0:T(1,128)} %fusion.1), calls=%async_computation.14 | async-start | bytes 524288 | tf_op jit(solution)/shard_map/all_to_all | solution.py:96
  506.8 152.1 %copy-start.15 = (pred[32]{0:T(512)(128)(4,1)S(1)}, pred[32]{0:T(512)(128)(4,1)}, u32[]{:S(2)}) copy-start(pred[32]{0:T(512)(128)(4,1)} %copy-done.11) | copy-start | bytes 100
  506.8 152.1 %copy-start.21 = (pred[32]{0:T(512)(128)(4,1)S(1)}, pred[32]{0:T(512)(128)(4,1)}, u32[]{:S(2)}) copy-start(pred[32]{0:T(512)(128)(4,1)} %copy-done.17) | copy-start | bytes 100
  506.9 9.9 %collective-permute-start.6 = (f32[7,2048]{1,0:T(8,128)S(1)}, f32[7,2048]{1,0:T(8,128)S(1)}, u32[]{:S(2)}, u32[]{:S(2)}) collective-permute-start(f32[7,2048]{1,0:T(8,128)S(1)} %broadcast_select_fusion.32), channel_id=1, source_target_pairs={{0,1},{1,2},{2,3},{3,0},{4,5},{5,6},{6,7},{7,4},{8,9},{9,10},{10,1... | collective-permute-start | bytes 172040 | tf_op jit(solution)/shard_map/ppermute | solution.py:22
  507.8 9.0 collective-permute-start.7
  692.8 4.4 collective-permute-start.8
  693.5 3.7 collective-permute-start.9
  697.2 43.8 %copy-start.25 = (f32[7,2048]{1,0:T(8,128)}, f32[7,2048]{1,0:T(8,128)S(1)}, u32[]{:S(2)}) copy-start(f32[7,2048]{1,0:T(8,128)S(1)} %collective-permute-done.8) | copy-start | bytes 172036
  740.9 23.5 %copy-start.31 = (f32[16]{0:T(128)S(1)}, f32[16]{0:T(128)}, u32[]{:S(2)}) copy-start(f32[16]{0:T(128)} %copy-done.29) | copy-start | bytes 196
  799.9 32.1 %all-to-all-start.20 = ((f32[32,7,2048]{2,1,0:T(8,128)}), f32[32,7,2048]{2,1,0:T(8,128)S(1)}, u32[]{:S(2)}, u32[]{:S(2)}) async-start(f32[32,7,2048]{2,1,0:T(8,128)} %select_add_fusion.1), calls=%async_computation.20 | async-start | bytes 4194304 | tf_op jit(solution)/shard_map/all_to_all | solution.py:48
  803.7 44.3 %copy-start.16 = (pred[32]{0:T(512)(128)(4,1)S(1)}, pred[32]{0:T(512)(128)(4,1)}, u32[]{:S(2)}) copy-start(pred[32]{0:T(512)(128)(4,1)} %copy-done.11) | copy-start | bytes 100
  803.7 44.3 %copy-start.22 = (pred[32]{0:T(512)(128)(4,1)S(1)}, pred[32]{0:T(512)(128)(4,1)}, u32[]{:S(2)}) copy-start(pred[32]{0:T(512)(128)(4,1)} %copy-done.17) | copy-start | bytes 100
  832.0 17.6 %all-to-all-start.23 = ((f32[32,1,256]{2,1,0:T(1,128)}), f32[32,1,256]{2,1,0:T(1,128)S(1)}, u32[]{:S(2)}, u32[]{:S(2)}) async-start(f32[32,1,256]{2,1,0:T(1,128)} %fusion.756), calls=%async_computation.23 | async-start | bytes 65536 | tf_op jit(solution)/shard_map/all_to_all | solution.py:97
  849.6 36.1 %all-to-all-start.21 = ((f32[32,7,2048]{2,1,0:T(8,128)}), f32[32,7,2048]{2,1,0:T(8,128)S(1)}, u32[]{:S(2)}, u32[]{:S(2)}) async-start(f32[32,7,2048]{2,1,0:T(8,128)} %select_add_fusion), calls=%async_computation.21 | async-start | bytes 4194304 | tf_op jit(solution)/shard_map/all_to_all | solution.py:48
  885.7 14.2 %all-to-all-start.22 = ((f32[32,1,2048]{2,1,0:T(1,128)}), f32[32,1,2048]{2,1,0:T(1,128)S(1)}, u32[]{:S(2)}, u32[]{:S(2)}) async-start(f32[32,1,2048]{2,1,0:T(1,128)} %fusion.2), calls=%async_computation.22 | async-start | bytes 524288 | tf_op jit(solution)/shard_map/all_to_all | solution.py:96
  892.2 10.0 %collective-permute-start.10 = (f32[7,2048]{1,0:T(8,128)S(1)}, f32[7,2048]{1,0:T(8,128)S(1)}, u32[]{:S(2)}, u32[]{:S(2)}) collective-permute-start(f32[7,2048]{1,0:T(8,128)S(1)} %broadcast_select_fusion.30), channel_id=1, source_target_pairs={{0,1},{1,2},{2,3},{3,0},{4,5},{5,6},{6,7},{7,4},{8,9},{9,10},{10,1... | collective-permute-start | bytes 172040 | tf_op jit(solution)/shard_map/ppermute | solution.py:22
  892.4 9.9 %collective-permute-start.11 = (f32[7,2048]{1,0:T(8,128)S(1)}, f32[7,2048]{1,0:T(8,128)S(1)}, u32[]{:S(2)}, u32[]{:S(2)}) collective-permute-start(f32[7,2048]{1,0:T(8,128)S(1)} %broadcast_select_fusion.24), channel_id=1, source_target_pairs={{1,0},{2,1},{3,2},{0,3},{5,4},{6,5},{7,6},{4,7},{9,8},{10,9},{11,1... | collective-permute-start | bytes 172040 | tf_op jit(solution)/shard_map/ppermute | solution.py:24
  (11 other events, 12.6 us)
where the time goes:
time: 993 us; the launch traced here: 980 us
  blocking collectives  385 us (39%)
  waiting for transfers between devices  234 us (24%)
  other arithmetic  226 us (23%)
  starting transfers between devices  106 us (11%)
  local copies, waits for them, and re-layouts  21.1 us (2%)
    all_to_all x9, waiting for transfers between devices, swap_faces(): lax.all_to_all(outgoing, 'bricks', split_axis=0, concat_axis=0, tiled=True)  215 us
    all_to_all x9, blocking collectives, swap_faces(): lax.all_to_all(outgoing, 'bricks', split_axis=0, concat_axis=0, tiled=True)  194 us
    psum x2, blocking collectives, global_squares(): return lax.psum(jnp.sum(values * values), ('bricks', 'slab'))  127 us
    add x12, other arithmetic, convolve(): summed = shifted if summed is None else summed + shifted  117 us
    psum x1, blocking collectives, shards(): lax.psum(jnp.sum(direction * applied), ('bricks', 'slab'))  64.5 us
    all_to_all x9, starting transfers between devices, swap_faces(): lax.all_to_all(outgoing, 'bricks', split_axis=0, concat_axis=0, tiled=True)  56.7 us
    reduce_sum x2, other arithmetic, shards(): jnp.sum(direction * applied)  22.7 us
    mul x2, other arithmetic, operate(): weighted = damping * damping * blurred  20.5 us
  transfers between devices with their start and end apart: 27, of which 16 were waited for; matrix products, arithmetic and copies ran while one was open for 7% of the time, Pallas kernels for 0%

commit v1 on v0

v1 whole, which is shorter than its diff:
```python
import jax
import jax.numpy as jnp
from jax import lax
from jax.experimental import pallas as pl
from jax.experimental.pallas import tpu as pltpu
from jax.sharding import PartitionSpec as P

NB = 32
ND = 128
TAPS = 15
REACH = 7
SHRINK = 0.5
WEIGHT = 0.3
MESH = pl.DeviceIdType.MESH
f32 = jnp.float32
bf16 = jnp.bfloat16

EXCHANGES = {
    "est": 2, "obs": 2, "t1": 2, "t2": 2, "t3": 2, "t4": 2, "t5": 4, "t6": 2, "t7": 4,
    "b0": 2, "b1": 2,
}
NAMES = list(EXCHANGES)


def kernel(slot, links, coords, taps, obs_ref, est_ref, sol_ref, res_ref, *scratch):
    n = len(NAMES)
    send = dict(zip(NAMES, scratch[:n]))
    recv = dict(zip(NAMES, scratch[n : 2 * n]))
    (fields, work, gathered, weights_hi, weights_lo, planes0, planes1, planes2, smooth_sum,
     damp, source, peers, row_of, send_sems, recv_sems, plane_send, plane_recv) = scratch[2 * n :]
    planes = (planes0, planes1, planes2)
    ssem = {name: send_sems.at[k] for k, name in enumerate(NAMES)}
    rsem = {name: recv_sems.at[k] for k, name in enumerate(NAMES)}

    my_row = lax.axis_index("bricks")
    my_slab = lax.axis_index("slab")
    me = my_row * 4 + my_slab
    my_z, my_y, my_core = my_row // 8, lax.rem(my_row // 2, 4), lax.rem(my_row, 2)
    slabs = [lax.rem(my_slab + d, 4) for d in range(4)]
    cores = [my_core, 1 - my_core]

    def far_first(j):
        return 2 + j - (j // 2) * (2 * j - 1)

    def everyone(visit):
        def group(step, carry):
            z = lax.rem(my_z + far_first(step // 4), 4)
            y = lax.rem(my_y + far_first(lax.rem(step, 4)), 4)
            for d in (2, 1, 3, 0):
                for c in (0, 1):
                    row = (z * 4 + y) * 2 + cores[c]
                    visit(row * 4 + slabs[d], (row, slabs[d]))
            return carry

        lax.fori_loop(0, 15, group, 0)
        for d in (2, 1, 3, 0):
            for c in (1, 0):
                if d or c:
                    row = (my_z * 4 + my_y) * 2 + cores[c]
                    visit(row * 4 + slabs[d], (row, slabs[d]))

    def start(name):
        rows = EXCHANGES[name]
        src, dst = send[name], recv[name]

        def part(ref, k):
            return ref.at[pl.ds(pl.multiple_of(rows * k, rows), rows)]

        def visit(number, device):
            pltpu.make_async_remote_copy(
                src_ref=part(src, number), dst_ref=part(dst, me), send_sem=ssem[name],
                recv_sem=rsem[name], device_id=device, device_id_type=MESH,
            ).start()

        everyone(visit)
        pltpu.make_async_copy(part(src, me), part(dst, me), rsem[name]).start()

    def arrive(name):
        dst = recv[name]
        pltpu.make_async_copy(dst, dst, rsem[name]).wait()

    barrier = pltpu.get_barrier_semaphore()

    def greet(number, device):
        pl.semaphore_signal(barrier, inc=1, device_id=device, device_id_type=MESH)

    everyone(greet)

    for h in range(2):
        block = est_ref[0, 8 * h : 8 * h + 8].reshape(128, 128)
        send["est"][pl.ds(h, 128, stride=2), :] = block.T
        send["obs"][pl.ds(h, 128, stride=2), :] = obs_ref[0, 8 * h : 8 * h + 8].reshape(128, 128)
    pl.semaphore_wait(barrier, ND - 1)
    start("est")

    zero = jnp.zeros((8, 128), f32)
    for ref in (fields.at[0], fields.at[1], fields.at[2], work,
                *(planes[op].at[side] for op in range(3) for side in range(2))):
        ref[NB] = zero

    def find_row(brick, carry):
        row = jnp.int32(0)
        for r in range(NB):
            row = jnp.where(slot[r] == brick, r, row)
        row_of[brick] = row
        return carry

    lax.fori_loop(0, NB, find_row, 0)

    def find_peers(row, carry):
        brick = slot[row]
        for k in range(6):
            link = links[brick, k]
            peers[row, k] = jnp.where(link >= 0, row_of[jnp.maximum(link, 0)], NB)
        return carry

    lax.fori_loop(0, NB, find_peers, 0)

    sub = lax.broadcasted_iota(jnp.int32, (8, 128), 0)
    lane = lax.broadcasted_iota(jnp.int32, (8, 128), 1)
    in_y = lax.rem(lane, 16)

    def make_weights(slot_at, axis, flipped):
        a = lax.broadcasted_iota(jnp.int32, (128, 128), 1)
        b = lax.broadcasted_iota(jnp.int32, (128, 128), 0)
        for side in range(3):
            if axis == 0:
                tap = 8 * (side - 1) + a // 16 - b // 16 + REACH
                fits = lax.rem(a, 16) == lax.rem(b, 16)
            elif axis == 1:
                tap = 16 * (side - 1) + lax.rem(a, 16) - lax.rem(b, 16) + REACH
                fits = a // 16 == b // 16
            else:
                tap = 128 * (side - 1) + a - b + REACH
                fits = a >= 0
            if flipped:
                tap = TAPS - 1 - tap
            tap = jnp.where(fits, tap, -1)

            def pick(t, total):
                return jnp.where(tap == t, taps[axis, t], total)

            block = lax.fori_loop(0, TAPS, pick, jnp.zeros((128, 128), f32))
            high = block.astype(bf16)
            low = (block - high.astype(f32)).astype(bf16)
            cols = pl.ds(128 * side, 128)
            weights_hi[slot_at, :, cols] = high
            weights_lo[slot_at, :, cols] = low

    make_weights(0, 0, False)
    make_weights(1, 1, False)

    def bricks_loop(body):
        def step(g, carry):
            for u in range(8):
                body(g * 8 + u)
            return carry

        lax.fori_loop(0, 4, step, 0)

    def gather(ref, axis):
        def body(b):
            own = ref[b]
            lower = ref[peers[b, 2 * axis]]
            upper = ref[peers[b, 2 * axis + 1]]
            if axis == 0:
                lower = pltpu.roll(jnp.where(sub == 7, lower, own), 1, 0)
                upper = pltpu.roll(jnp.where(sub == 0, upper, own), 7, 0)
            gathered[b, :, 0:128] = lower
            gathered[b, :, 128:256] = own
            gathered[b, :, 256:384] = upper

        bricks_loop(body)

    def split(values):
        high = values.astype(bf16)
        return high, (values - high.astype(f32)).astype(bf16)

    NT = (((1,), (1,)), ((), ()))

    def apply(ref, axis, which):
        gather(ref, axis)
        high, low = split(gathered[...].reshape(256, 384))
        w_high, w_low = weights_hi[which], weights_lo[which]
        return (
            lax.dot_general(high, w_high, NT, preferred_element_type=f32)
            + lax.dot_general(low, w_high, NT, preferred_element_type=f32)
            + lax.dot_general(high, w_low, NT, preferred_element_type=f32)
        )

    def apply_turned(ref, axis, which):
        gather(ref, axis)
        high, low = split(gathered[...].reshape(256, 384))
        w_high, w_low = weights_hi[which], weights_lo[which]
        return (
            lax.dot_general(w_high, high, NT, preferred_element_type=f32)
            + lax.dot_general(w_high, low, NT, preferred_element_type=f32)
            + lax.dot_general(w_low, high, NT, preferred_element_type=f32)
        )

    def post(name, turned):
        rows = EXCHANGES[name]
        for h in range(2):
            send[name][pl.ds(h, 128, stride=rows), :] = turned[:, 128 * h : 128 * h + 128]

    def unpack(name, ref):
        rows = EXCHANGES[name]
        for h in range(2):
            block = recv[name][pl.ds(h, 128, stride=rows), :].T
            ref[16 * h : 16 * h + 16] = block.reshape(16, 8, 128)

    def plane_copies(op):
        copies = []
        for side, shift in ((0, 1), (1, ND - 1)):
            other = lax.rem(me + shift, ND)
            copies.append(
                pltpu.make_async_remote_copy(
                    src_ref=fields.at[op, pl.ds(0, NB)],
                    dst_ref=planes[op].at[side, pl.ds(0, NB)],
                    send_sem=plane_send.at[op, side], recv_sem=plane_recv.at[op, side],
                    device_id=(other // 4, lax.rem(other, 4)), device_id_type=MESH,
                )
            )
        return copies

    def around(op, b):
        field = fields.at[op]
        own = field[b]
        z_low, z_high, y_low, y_high = (field[peers[b, k]] for k in range(4))
        down = pltpu.roll(jnp.where(sub == 7, z_low, own), 1, 0)
        up = pltpu.roll(jnp.where(sub == 0, z_high, own), 7, 0)
        before_z = pltpu.roll(jnp.where(lane >= 112, down, own), 16, 1)
        beyond_z = pltpu.roll(jnp.where(lane < 16, up, own), 112, 1)
        before_y = pltpu.roll(jnp.where(in_y == 15, pltpu.roll(y_low, 112, 1), own), 1, 1)
        beyond_y = pltpu.roll(jnp.where(in_y == 0, pltpu.roll(y_high, 16, 1), own), 127, 1)
        before_x = planes[op][0, jnp.where(me == 0, peers[b, 4], b)]
        beyond_x = planes[op][1, jnp.where(me == ND - 1, peers[b, 5], b)]
        has = [jnp.where(peers[b, 2 * k] < NB, 1.0, 0.0) for k in range(3)]
        low_z = jnp.where((sub == 0) & (lane < 16), has[0], 1.0)
        low_y = jnp.where(in_y == 0, has[1], 1.0)
        low_x = jnp.where(me == 0, has[2], 1.0)
        return own, ((before_z, beyond_z, low_z), (before_y, beyond_y, low_y),
                     (before_x, beyond_x, low_x))

    def smooth_shrunk(op):
        def penalty(g):
            return -SHRINK * g / (g * g + SHRINK)

        def body(b):
            own, sides = around(op, b)
            total = zero
            for before, beyond, low in sides:
                total = total + penalty(own - before) * low - penalty(beyond - own)
            smooth_sum[b] = WEIGHT * total

        bricks_loop(body)

    def smooth_linear(op):
        def body(b):
            own, sides = around(op, b)
            total = zero
            for before, beyond, low in sides:
                total = total + (own - before) * low - (beyond - own)
            smooth_sum[b] = WEIGHT * total

        bricks_loop(body)

    def operate(op, out, to_zy, to_x, first, note=None, before_x=None, meanwhile=None):
        planes_moving = plane_copies(op)
        work[0:NB] = apply(fields.at[op], 0, 0).reshape(NB, 8, 128)
        post(to_zy, apply_turned(work, 1, 1))
        if note is not None:
            note()
        start(to_zy)
        for copy in planes_moving:
            copy.start()
        if before_x is not None:
            before_x()
        arrive(to_zy)
        unpack(to_zy, work)
        blurred = apply(work, 2, 2).reshape(NB, 8, 128)
        weighted = damp[...] * damp[...] * blurred
        work[0:NB] = source[...] - weighted if first else weighted
        post(to_x, apply_turned(work, 2, 3))
        start(to_x)
        for copy in planes_moving:
            copy.wait()
        if first:
            smooth_shrunk(op)
        else:
            smooth_linear(op)
        if meanwhile is not None:
            meanwhile()
        arrive(to_x)
        unpack(to_x, work)
        work[0:NB] = apply(work, 1, 4).reshape(NB, 8, 128)
        return apply(work, 0, 5).reshape(NB, 8, 128) + smooth_sum[...]

    arrive("est")
    fields[0, 0:NB] = recv["est"][...].reshape(NB, 8, 128)

    def prepare():
        start("obs")
        make_weights(2, 2, False)
        make_weights(3, 2, True)

        def body(b):
            depth = coords[slot[b], 0] * 64 + 8 * sub + me // 16
            damp[b] = jnp.exp(-depth.astype(f32) / 256.0)

        bricks_loop(body)
        arrive("obs")
        source[...] = damp[...] * recv["obs"][...].reshape(NB, 8, 128)

    def prepare_adjoint():
        make_weights(4, 1, True)
        make_weights(5, 0, True)

    fields[1, 0:NB] = operate(0, 1, "t1", "t2", True, before_x=prepare, meanwhile=prepare_adjoint)

    def send_r0():
        send["b0"][...] = fields[1, 0:NB].reshape(256, 128)
        start("b0")

    fields[2, 0:NB] = operate(1, 2, "t3", "t4", False, before_x=send_r0)

    def note_sums():
        r0, w1 = fields[1, 0:NB].reshape(256, 128), fields[2, 0:NB].reshape(256, 128)
        for k, product in ((2, r0 * r0), (3, r0 * w1)):
            total = jnp.sum(product, axis=0, keepdims=True)
            send["t5"][pl.ds(k, 128, stride=4), :] = jnp.broadcast_to(total, (128, 128))

    def send_w1():
        send["b1"][...] = fields[2, 0:NB].reshape(256, 128)
        start("b1")

    w2 = operate(2, None, "t5", "t6", False, note=note_sums, before_x=send_w1).reshape(256, 128)

    def total_of(rows):
        return jnp.sum(rows, keepdims=True)

    rr = total_of(recv["t5"][pl.ds(2, 128, stride=4), :])
    r0w1 = total_of(recv["t5"][pl.ds(3, 128, stride=4), :])
    step1 = rr / r0w1

    work[0:NB] = w2.reshape(NB, 8, 128)
    r0, w1 = fields[1, 0:NB].reshape(256, 128), fields[2, 0:NB].reshape(256, 128)
    r1 = r0 - step1 * w1
    ar1 = w1 - step1 * w2
    low_half = lax.broadcasted_iota(jnp.int32, (1, 128), 1) < 64

    def two_sums(first, second):
        a = jnp.sum(first, axis=0, keepdims=True)
        b = jnp.sum(second, axis=0, keepdims=True)
        a = a + pltpu.roll(a, 64, 1)
        b = b + pltpu.roll(b, 64, 1)
        return jnp.broadcast_to(jnp.where(low_half, a, b), (128, 128))

    w2_rows = w2.reshape(128, 2, 128)
    for h in range(2):
        send["t7"][pl.ds(h, 128, stride=4), :] = w2_rows[:, h, :]
    send["t7"][pl.ds(2, 128, stride=4), :] = two_sums(r1 * r1, r1 * ar1)
    send["t7"][pl.ds(3, 128, stride=4), :] = two_sums(r1 * w1, r0 * ar1)
    start("t7")
    arrive("b0")
    arrive("b1")
    arrive("t7")
    low = lax.broadcasted_iota(jnp.int32, (128, 128), 1) < 64
    row2 = recv["t7"][pl.ds(2, 128, stride=4), :]
    row3 = recv["t7"][pl.ds(3, 128, stride=4), :]
    rr1 = total_of(jnp.where(low, row2, 0.0))
    r1ar1 = total_of(jnp.where(low, 0.0, row2))
    cross = total_of(row3)
    ratio = rr1 / rr
    step2 = rr1 / (r1ar1 + ratio * cross + ratio * ratio * r0w1)
    for h in range(2):
        b0 = recv["b0"][pl.ds(h, 128, stride=2), :].T
        b1 = recv["b1"][pl.ds(h, 128, stride=2), :].T
        b2 = recv["t7"][pl.ds(h, 128, stride=4), :].T
        r = b0 - step1 * b1
        ar = b1 - step1 * b2
        est = est_ref[0, 8 * h : 8 * h + 8].reshape(128, 128)
        sol = est + step1 * b0 + step2 * (r + ratio * b0)
        res = r - step2 * (ar + ratio * b1)
        sol_ref[0, 8 * h : 8 * h + 8] = sol.reshape(8, 16, 128)
        res_ref[0, 8 * h : 8 * h + 8] = res.reshape(8, 16, 128)

    for name in NAMES:
        sent = send[name].at[pl.ds(0, 127 * EXCHANGES[name])]
        pltpu.make_async_copy(sent, sent, ssem[name]).wait()


def shards(observed, estimate, blur_taps, slot_brick, neighbours, coords):
    smem = pl.BlockSpec(memory_space=pltpu.SMEM)
    vmem = pl.BlockSpec(memory_space=pltpu.VMEM)
    shape = jax.ShapeDtypeStruct(estimate.shape, f32)
    buffers = [pltpu.VMEM((ND * EXCHANGES[name], 128), f32) for name in NAMES]
    count = len(NAMES)
    return pl.pallas_call(
        kernel,
        out_shape=(shape, shape),
        in_specs=[smem] * 4 + [vmem] * 2,
        out_specs=(vmem, vmem),
        scratch_shapes=buffers + buffers + [
            pltpu.VMEM((3, NB + 1, 8, 128), f32),
            pltpu.VMEM((NB + 1, 8, 128), f32),
            pltpu.VMEM((NB, 8, 384), f32),
            pltpu.VMEM((6, 128, 384), bf16),
            pltpu.VMEM((6, 128, 384), bf16),
            *[pltpu.VMEM((2, NB + 1, 8, 128), f32)] * 3,
            pltpu.VMEM((NB, 8, 128), f32),
            pltpu.VMEM((NB, 8, 128), f32),
            pltpu.VMEM((NB, 8, 128), f32),
            pltpu.SMEM((NB, 6), jnp.int32),
            pltpu.SMEM((NB,), jnp.int32),
            pltpu.SemaphoreType.DMA((count,)),
            pltpu.SemaphoreType.DMA((count,)),
            pltpu.SemaphoreType.DMA((3, 2)),
            pltpu.SemaphoreType.DMA((3, 2)),
        ],
        compiler_params=pltpu.CompilerParams(collective_id=0, has_side_effects=True),
        name="splitting_step",
    )(slot_brick, neighbours, coords, blur_taps, observed, estimate)


def solution(mesh):
    split = P("bricks", "slab", None, None)
    return jax.shard_map(
        shards,
        mesh=mesh,
        in_specs=(split, split, P(), P(), P(), P()),
        out_specs=(split, split),
        check_vma=False,
    )
```

time: 993 us -> 83.5 us (0.08); the launches traced: 980 us -> 83.3 us
  blocking collectives: 385 us -> 0 us
  waiting for transfers between devices: 234 us -> 0 us
  other arithmetic: 226 us -> 0 us
  starting transfers between devices: 106 us -> 0 us
  Pallas kernels: 0 us -> 78.3 us
  local copies, waits for them, and re-layouts: 21.1 us -> 4.34 us
    all_to_all x15 -> x0, waiting for transfers between devices: 230 us -> none  [the longest x9 215 us: swap_faces(): lax.all_to_all(outgoing, 'bricks', split_axis=0, concat_axis=0, tiled=True)]
    all_to_all x9 -> x0, blocking collectives: 194 us -> none  [swap_faces(): lax.all_to_all(outgoing, 'bricks', split_axis=0, concat_axis=0, tiled=True)]
    psum x3 -> x0, blocking collectives: 192 us -> none  [the longest x2 127 us: global_squares(): return lax.psum(jnp.sum(values * values), ('bricks', 'slab'))]
    add x38 -> x0, other arithmetic: 149 us -> none  [the longest x12 117 us: convolve(): summed = shifted if summed is None else summed + shifted]
    all_to_all x15 -> x0, starting transfers between devices: 88.9 us -> none  [the longest x9 56.7 us: swap_faces(): lax.all_to_all(outgoing, 'bricks', split_axis=0, concat_axis=0, tiled=True)]
    pallas_call x0 -> x1, Pallas kernels: none -> 78.3 us  [shards(): pl.pallas_call(kernel, out_shape=(shape, shape), in_specs=[smem] * 4 + [v...]
    reduce_sum x32 -> x0, other arithmetic: 38.2 us -> none  [the longest x2 22.7 us: shards(): jnp.sum(direction * applied)]
    mul x2 -> x0, other arithmetic: 20.5 us -> none  [operate(): weighted = damping * damping * blurred]
  transfers between devices with their start and end apart: 27 -> 0, of which waited for: 16 -> 0; matrix products, arithmetic and copies ran while one was open for 7% -> 0% of each run, Pallas kernels for 0% -> 0%
where the time goes in v1:
time: 83.5 us; the launch traced here: 83.3 us
  Pallas kernels  78.3 us (94%)
  local copies, waits for them, and re-layouts  4.34 us (5%)
    pallas_call x1, Pallas kernels, shards(): pl.pallas_call(kernel, out_shape=(shape, shape), in_specs=[smem] * 4 + [v...  78.3 us
    unnamed x8, local copies, waits for them, and re-layouts  4.34 us

profile of v1, /device:TPU:1, one launch (start us, length us, event | category | flops | bytes accessed | tf_op | source)
XLA Modules:
  0.0 83.3 jit_solution(1744358206321585289)
XLA Ops:
  0.6 0.0 copy-start.1
  0.6 1.4 %copy.8.links = s32[32,6]{1,0:T(8,128)} copy(s32[32,6]{0,1:T(8,128)} %param.10) | data formatting | bytes 1536 | tf_op args[4]
  2.0 0.0 copy-done.1
  2.0 0.7 copy.9.coords
  2.7 78.3 %splitting_step.1 = (f32[1,16,16,128]{3,2,1,0:T(8,128)}, f32[1,16,16,128]{3,2,1,0:T(8,128)}) custom-call(s32[32]{0:T(128)} %slot.1, s32[32,6]{1,0:T(8,128)} %copy.8.links, s32[32,3]{1,0:T(8,128)} %copy.9.coords, f32[3,15]{1,0:T(4,128)} %taps.1, f32[1,16,16,128]{3,2,1,0:T(8,128)} %obs_ref.1, f32[1,16,16,128]{3,2,1,0:T(8,128)} %est_ref.1), custom_call_target="tpu_custom_call" | custom-call | tf_op jit(solution)/shard_map/splitting_step/pallas_call | solution.py:399
  81.0 0.0 copy-start
  81.0 1.6 %copy.12 = f32[1,16,16,128]{3,2,1,0:T(8,128)} copy(f32[1,16,16,128]{3,2,1,0:T(8,128)} %get-tuple-element.4) | data formatting | bytes 262144
  82.6 0.0 copy-done
  82.6 0.7 copy.13
Async XLA Ops:
  0.6 1.4 %copy-start.1 = (s32[32,3]{0,1:T(4,128)S(1)}, s32[32,3]{0,1:T(4,128)}, u32[]{:S(2)}) copy-start(s32[32,3]{0,1:T(4,128)} %param.11) | copy-start | bytes 1156
  81.0 1.6 %copy-start = (f32[1,16,16,128]{3,2,1,0:T(8,128)S(1)}, f32[1,16,16,128]{3,2,1,0:T(8,128)}, u32[]{:S(2)}) copy-start(f32[1,16,16,128]{3,2,1,0:T(8,128)} %get-tuple-element.5) | copy-start | bytes 393220

commit v2 on v1

--- a/solution.py
+++ b/solution.py
@@ -16,25 +16,28 @@
 bf16 = jnp.bfloat16
 
 EXCHANGES = {
-    "est": 2, "obs": 2, "t1": 2, "t2": 2, "t3": 2, "t4": 2, "t5": 4, "t6": 2, "t7": 4,
-    "b0": 2, "b1": 2,
+    "est": (2, 2, "from"), "obs": (2, 2, "from"), "t1": (2, 2, ""), "t2": (2, 2, ""),
+    "t3": (2, 2, ""), "t4": (2, 2, ""), "t5": (2, 2, ""), "t6": (2, 2, ""),
+    "t7": (3, 4, "to"), "b0": (2, 2, "to"), "b1": (2, 2, "to"), "sums": (1, 1, ""),
 }
 NAMES = list(EXCHANGES)
 
 
-def kernel(slot, links, coords, taps, obs_ref, est_ref, sol_ref, res_ref, *scratch):
+def kernel(slot_in, links_in, coords_in, taps_in, obs_in, est_in, sol_ref, res_ref, *scratch):
     n = len(NAMES)
     send = dict(zip(NAMES, scratch[:n]))
     recv = dict(zip(NAMES, scratch[n : 2 * n]))
     (fields, work, gathered, weights_hi, weights_lo, planes0, planes1, planes2, smooth_sum,
-     damp, source, peers, row_of, send_sems, recv_sems, plane_send, plane_recv) = scratch[2 * n :]
+     damp, source, peers, row_of, send_sems, recv_sems, plane_send, plane_recv, slot, links,
+     coords, taps, obs_ref, est_ref, load_sems) = scratch[2 * n :]
     planes = (planes0, planes1, planes2)
     ssem = {name: send_sems.at[k] for k, name in enumerate(NAMES)}
     rsem = {name: recv_sems.at[k] for k, name in enumerate(NAMES)}
 
     my_row = lax.axis_index("bricks")
     my_slab = lax.axis_index("slab")
-    me = my_row * 4 + my_slab
+    me = my_row // 2 * 8 + my_slab * 2 + lax.rem(my_row, 2)
+    my_brick = my_row * 4 + my_slab
     my_z, my_y, my_core = my_row // 8, lax.rem(my_row // 2, 4), lax.rem(my_row, 2)
     slabs = [lax.rem(my_slab + d, 4) for d in range(4)]
     cores = [my_core, 1 - my_core]
@@ -49,7 +52,8 @@
             for d in (2, 1, 3, 0):
                 for c in (0, 1):
                     row = (z * 4 + y) * 2 + cores[c]
-                    visit(row * 4 + slabs[d], (row, slabs[d]))
+                    number = ((z * 4 + y) * 4 + slabs[d]) * 2 + cores[c]
+                    visit(number, row * 4 + slabs[d], (row, slabs[d]))
             return carry
 
         lax.fori_loop(0, 15, group, 0)
@@ -57,41 +61,57 @@
             for c in (1, 0):
                 if d or c:
                     row = (my_z * 4 + my_y) * 2 + cores[c]
-                    visit(row * 4 + slabs[d], (row, slabs[d]))
+                    number = ((my_z * 4 + my_y) * 4 + slabs[d]) * 2 + cores[c]
+                    visit(number, row * 4 + slabs[d], (row, slabs[d]))
 
     def start(name):
-        rows = EXCHANGES[name]
+        rows, pitch, bricks = EXCHANGES[name]
         src, dst = send[name], recv[name]
+        from_me = my_brick if bricks == "from" else me
+        to_me = my_brick if bricks == "to" else me
 
         def part(ref, k):
-            return ref.at[pl.ds(pl.multiple_of(rows * k, rows), rows)]
-
-        def visit(number, device):
+            return ref.at[pl.ds(pl.multiple_of(pitch * k, pitch), rows)]
+
+        def visit(number, place, device):
             pltpu.make_async_remote_copy(
-                src_ref=part(src, number), dst_ref=part(dst, me), send_sem=ssem[name],
-                recv_sem=rsem[name], device_id=device, device_id_type=MESH,
+                src_ref=part(src, place if bricks == "to" else number),
+                dst_ref=part(dst, from_me), send_sem=ssem[name], recv_sem=rsem[name],
+                device_id=device, device_id_type=MESH,
             ).start()
 
         everyone(visit)
-        pltpu.make_async_copy(part(src, me), part(dst, me), rsem[name]).start()
+        pltpu.make_async_copy(part(src, to_me), part(dst, from_me), rsem[name]).start()
 
     def arrive(name):
-        dst = recv[name]
+        dst = recv[name].at[pl.ds(0, ND * EXCHANGES[name][0])]
         pltpu.make_async_copy(dst, dst, rsem[name]).wait()
 
     barrier = pltpu.get_barrier_semaphore()
 
-    def greet(number, device):
+    def greet(number, place, device):
         pl.semaphore_signal(barrier, inc=1, device_id=device, device_id_type=MESH)
 
     everyone(greet)
-
+    loads = [
+        pltpu.make_async_copy(src, dst, load_sems.at[k])
+        for k, (src, dst) in enumerate(
+            ((est_in, est_ref), (obs_in, obs_ref), (slot_in, slot), (links_in, links),
+             (coords_in, coords), (taps_in, taps)))
+    ]
+    for load in loads:
+        load.start()
+    for load in loads[:2]:
+        load.wait()
     for h in range(2):
         block = est_ref[0, 8 * h : 8 * h + 8].reshape(128, 128)
         send["est"][pl.ds(h, 128, stride=2), :] = block.T
         send["obs"][pl.ds(h, 128, stride=2), :] = obs_ref[0, 8 * h : 8 * h + 8].reshape(128, 128)
     pl.semaphore_wait(barrier, ND - 1)
     start("est")
+    start("obs")
+    for load in loads[2:]:
+        load.wait()
 
     zero = jnp.zeros((8, 128), f32)
     for ref in (fields.at[0], fields.at[1], fields.at[2], work,
@@ -110,7 +130,7 @@
     def find_peers(row, carry):
         brick = slot[row]
         for k in range(6):
-            link = links[brick, k]
+            link = links[k, brick]
             peers[row, k] = jnp.where(link >= 0, row_of[jnp.maximum(link, 0)], NB)
         return carry
 
@@ -199,12 +219,12 @@
         )
 
     def post(name, turned):
-        rows = EXCHANGES[name]
+        rows = EXCHANGES[name][1]
         for h in range(2):
             send[name][pl.ds(h, 128, stride=rows), :] = turned[:, 128 * h : 128 * h + 128]
 
     def unpack(name, ref):
-        rows = EXCHANGES[name]
+        rows = EXCHANGES[name][1]
         for h in range(2):
             block = recv[name][pl.ds(h, 128, stride=rows), :].T
             ref[16 * h : 16 * h + 16] = block.reshape(16, 8, 128)
@@ -213,12 +233,14 @@
         copies = []
         for side, shift in ((0, 1), (1, ND - 1)):
             other = lax.rem(me + shift, ND)
+            chip, core = other // 2, lax.rem(other, 2)
             copies.append(
                 pltpu.make_async_remote_copy(
                     src_ref=fields.at[op, pl.ds(0, NB)],
                     dst_ref=planes[op].at[side, pl.ds(0, NB)],
                     send_sem=plane_send.at[op, side], recv_sem=plane_recv.at[op, side],
-                    device_id=(other // 4, lax.rem(other, 4)), device_id_type=MESH,
+                    device_id=(chip // 4 * 2 + core, lax.rem(chip, 4)),
+                    device_id_type=MESH,
                 )
             )
         return copies
@@ -265,15 +287,13 @@
 
         bricks_loop(body)
 
-    def operate(op, out, to_zy, to_x, first, note=None, before_x=None, meanwhile=None):
+    def operate(op, out, to_zy, to_x, first, before_x=None, meanwhile=None):
         planes_moving = plane_copies(op)
+        for copy in planes_moving:
+            copy.start()
         work[0:NB] = apply(fields.at[op], 0, 0).reshape(NB, 8, 128)
         post(to_zy, apply_turned(work, 1, 1))
-        if note is not None:
-            note()
         start(to_zy)
-        for copy in planes_moving:
-            copy.start()
         if before_x is not None:
             before_x()
         arrive(to_zy)
@@ -300,12 +320,11 @@
     fields[0, 0:NB] = recv["est"][...].reshape(NB, 8, 128)
 
     def prepare():
-        start("obs")
         make_weights(2, 2, False)
         make_weights(3, 2, True)
 
         def body(b):
-            depth = coords[slot[b], 0] * 64 + 8 * sub + me // 16
+            depth = coords[0, slot[b]] * 64 + 8 * sub + me // 16
             damp[b] = jnp.exp(-depth.astype(f32) / 256.0)
 
         bricks_loop(body)
@@ -324,29 +343,6 @@
 
     fields[2, 0:NB] = operate(1, 2, "t3", "t4", False, before_x=send_r0)
 
-    def note_sums():
-        r0, w1 = fields[1, 0:NB].reshape(256, 128), fields[2, 0:NB].reshape(256, 128)
-        for k, product in ((2, r0 * r0), (3, r0 * w1)):
-            total = jnp.sum(product, axis=0, keepdims=True)
-            send["t5"][pl.ds(k, 128, stride=4), :] = jnp.broadcast_to(total, (128, 128))
-
-    def send_w1():
-        send["b1"][...] = fields[2, 0:NB].reshape(256, 128)
-        start("b1")
-
-    w2 = operate(2, None, "t5", "t6", False, note=note_sums, before_x=send_w1).reshape(256, 128)
-
-    def total_of(rows):
-        return jnp.sum(rows, keepdims=True)
-
-    rr = total_of(recv["t5"][pl.ds(2, 128, stride=4), :])
-    r0w1 = total_of(recv["t5"][pl.ds(3, 128, stride=4), :])
-    step1 = rr / r0w1
-
-    work[0:NB] = w2.reshape(NB, 8, 128)
-    r0, w1 = fields[1, 0:NB].reshape(256, 128), fields[2, 0:NB].reshape(256, 128)
-    r1 = r0 - step1 * w1
-    ar1 = w1 - step1 * w2
     low_half = lax.broadcasted_iota(jnp.int32, (1, 128), 1) < 64
 
     def two_sums(first, second):
@@ -354,23 +350,50 @@
         b = jnp.sum(second, axis=0, keepdims=True)
         a = a + pltpu.roll(a, 64, 1)
         b = b + pltpu.roll(b, 64, 1)
-        return jnp.broadcast_to(jnp.where(low_half, a, b), (128, 128))
-
+        return jnp.where(low_half, a, b)
+
+    def send_w1():
+        r0, w1 = fields[1, 0:NB].reshape(256, 128), fields[2, 0:NB].reshape(256, 128)
+        send["sums"][...] = jnp.broadcast_to(two_sums(r0 * r0, r0 * w1), (128, 128))
+        start("sums")
+        send["b1"][...] = w1
+        start("b1")
+
+    w2 = operate(2, None, "t5", "t6", False, before_x=send_w1).reshape(256, 128)
+
+    def total_of(rows):
+        return jnp.sum(rows, keepdims=True)
+
+    low = lax.broadcasted_iota(jnp.int32, (128, 128), 1) < 64
+    arrive("sums")
+    rr = total_of(jnp.where(low, recv["sums"][...], 0.0))
+    r0w1 = total_of(jnp.where(low, 0.0, recv["sums"][...]))
+    step1 = rr / r0w1
+
+    work[0:NB] = w2.reshape(NB, 8, 128)
+    r0, w1 = fields[1, 0:NB].reshape(256, 128), fields[2, 0:NB].reshape(256, 128)
+    r1 = r0 - step1 * w1
+    ar1 = w1 - step1 * w2
+    first_pair = two_sums(r1 * r1, r1 * ar1)
+    second_pair = two_sums(r1 * w1, r0 * ar1)
+    quarter = lax.rem(lax.broadcasted_iota(jnp.int32, (1, 128), 1), 64) < 32
+    first_pair = first_pair + pltpu.roll(first_pair, 96, 1)
+    second_pair = second_pair + pltpu.roll(second_pair, 32, 1)
+    sums = jnp.where(quarter, first_pair, second_pair)
     w2_rows = w2.reshape(128, 2, 128)
     for h in range(2):
         send["t7"][pl.ds(h, 128, stride=4), :] = w2_rows[:, h, :]
-    send["t7"][pl.ds(2, 128, stride=4), :] = two_sums(r1 * r1, r1 * ar1)
-    send["t7"][pl.ds(3, 128, stride=4), :] = two_sums(r1 * w1, r0 * ar1)
+    send["t7"][pl.ds(2, 128, stride=4), :] = jnp.broadcast_to(sums, (128, 128))
     start("t7")
     arrive("b0")
     arrive("b1")
     arrive("t7")
-    low = lax.broadcasted_iota(jnp.int32, (128, 128), 1) < 64
-    row2 = recv["t7"][pl.ds(2, 128, stride=4), :]
-    row3 = recv["t7"][pl.ds(3, 128, stride=4), :]
-    rr1 = total_of(jnp.where(low, row2, 0.0))
-    r1ar1 = total_of(jnp.where(low, 0.0, row2))
-    cross = total_of(row3)
+    sums = recv["t7"][pl.ds(2, 128, stride=4), :]
+    lane_of = lax.broadcasted_iota(jnp.int32, (128, 128), 1)
+    own = lax.rem(lane_of, 64) < 32
+    rr1 = total_of(jnp.where(own & low, sums, 0.0))
+    r1ar1 = total_of(jnp.where(own & (lane_of >= 64), sums, 0.0))
+    cross = total_of(jnp.where(own, 0.0, sums))
     ratio = rr1 / rr
     step2 = rr1 / (r1ar1 + ratio * cross + ratio * ratio * r0w1)
     for h in range(2):
@@ -386,20 +409,20 @@
         res_ref[0, 8 * h : 8 * h + 8] = res.reshape(8, 16, 128)
 
     for name in NAMES:
-        sent = send[name].at[pl.ds(0, 127 * EXCHANGES[name])]
+        sent = send[name].at[pl.ds(0, (ND - 1) * EXCHANGES[name][0])]
         pltpu.make_async_copy(sent, sent, ssem[name]).wait()
 
 
 def shards(observed, estimate, blur_taps, slot_brick, neighbours, coords):
-    smem = pl.BlockSpec(memory_space=pltpu.SMEM)
+    place = pl.BlockSpec(memory_space=pl.ANY)
     vmem = pl.BlockSpec(memory_space=pltpu.VMEM)
     shape = jax.ShapeDtypeStruct(estimate.shape, f32)
-    buffers = [pltpu.VMEM((ND * EXCHANGES[name], 128), f32) for name in NAMES]
+    buffers = [pltpu.VMEM((ND * EXCHANGES[name][1], 128), f32) for name in NAMES]
     count = len(NAMES)
     return pl.pallas_call(
         kernel,
         out_shape=(shape, shape),
-        in_specs=[smem] * 4 + [vmem] * 2,
+        in_specs=[place] * 6,
         out_specs=(vmem, vmem),
         scratch_shapes=buffers + buffers + [
             pltpu.VMEM((3, NB + 1, 8, 128), f32),
@@ -417,10 +440,17 @@
             pltpu.SemaphoreType.DMA((count,)),
             pltpu.SemaphoreType.DMA((3, 2)),
             pltpu.SemaphoreType.DMA((3, 2)),
+            pltpu.SMEM((NB,), jnp.int32),
+            pltpu.SMEM((6, NB), jnp.int32),
+            pltpu.SMEM((3, NB), jnp.int32),
+            pltpu.SMEM((3, TAPS), f32),
+            pltpu.VMEM(observed.shape, f32),
+            pltpu.VMEM(estimate.shape, f32),
+            pltpu.SemaphoreType.DMA((6,)),
         ],
         compiler_params=pltpu.CompilerParams(collective_id=0, has_side_effects=True),
         name="splitting_step",
-    )(slot_brick, neighbours, coords, blur_taps, observed, estimate)
+    )(slot_brick, neighbours.T, coords.T, blur_taps, observed, estimate)
 
 
 def solution(mesh):

time: 83.5 us -> 77.9 us (0.933)
  Pallas kernels: 78.3 us -> 74.9 us
  local copies, waits for them, and re-layouts: 4.34 us -> 2.26 us
    pallas_call x1, Pallas kernels: 78.3 us -> 74.9 us  [shards(): pl.pallas_call(kernel, out_shape=(shape, shape), in_specs=[place] * 6, ou...]
    unnamed x8 -> x4, local copies, waits for them, and re-layouts: 4.34 us -> 2.26 us
where the time goes in v2:
time: 77.9 us; the launch traced here: 77.8 us
  Pallas kernels  74.9 us (96%)
  local copies, waits for them, and re-layouts  2.26 us (3%)
    pallas_call x1, Pallas kernels, shards(): pl.pallas_call(kernel, out_shape=(shape, shape), in_specs=[place] * 6, ou...  74.9 us
    unnamed x4, local copies, waits for them, and re-layouts  2.26 us

profile of v2, /device:TPU:1, one launch (start us, length us, event | category | flops | bytes accessed | tf_op | source)
XLA Modules:
  0.0 77.8 jit_solution(945424948212748253)
XLA Ops:
  0.6 74.9 %splitting_step.1 = (f32[1,16,16,128]{3,2,1,0:T(8,128)}, f32[1,16,16,128]{3,2,1,0:T(8,128)}) custom-call(s32[32]{0:T(128)} %slot_in.1, s32[6,32]{1,0:T(8,128)} %bitcast.2, s32[3,32]{1,0:T(4,128)} %bitcast.3, f32[3,15]{1,0:T(4,128)} %taps_in.1, f32[1,16,16,128]{3,2,1,0:T(8,128)} %obs_in.1, f32[1,16,16,128]{3,2,1,0:T(8,128)} %est_in.1), custom_call_target="tpu_custom_call" | custom-call | tf_op jit(solution)/shard_map/splitting_step/pallas_call | solution.py:422
  75.5 0.0 copy-start
  75.5 1.6 %copy.10 = f32[1,16,16,128]{3,2,1,0:T(8,128)} copy(f32[1,16,16,128]{3,2,1,0:T(8,128)} %get-tuple-element.4) | data formatting | bytes 262144
  77.1 0.0 copy-done
  77.1 0.7 copy.11
Async XLA Ops:
  75.5 1.6 %copy-start = (f32[1,16,16,128]{3,2,1,0:T(8,128)S(1)}, f32[1,16,16,128]{3,2,1,0:T(8,128)}, u32[]{:S(2)}) copy-start(f32[1,16,16,128]{3,2,1,0:T(8,128)} %get-tuple-element.5) | copy-start | bytes 393220

commit v3 on v2

--- a/solution.py
+++ b/solution.py
@@ -18,7 +18,8 @@
 EXCHANGES = {
     "est": (2, 2, "from"), "obs": (2, 2, "from"), "t1": (2, 2, ""), "t2": (2, 2, ""),
     "t3": (2, 2, ""), "t4": (2, 2, ""), "t5": (2, 2, ""), "t6": (2, 2, ""),
-    "t7": (3, 4, "to"), "b0": (2, 2, "to"), "b1": (2, 2, "to"), "sums": (1, 1, ""),
+    "t7": (2, 2, "to"), "b0": (2, 2, "to"), "b1": (2, 2, "to"), "sums1": (1, 1, ""),
+    "sums2": (1, 1, ""),
 }
 NAMES = list(EXCHANGES)
 
@@ -27,9 +28,9 @@
     n = len(NAMES)
     send = dict(zip(NAMES, scratch[:n]))
     recv = dict(zip(NAMES, scratch[n : 2 * n]))
-    (fields, work, gathered, weights_hi, weights_lo, planes0, planes1, planes2, smooth_sum,
+    (fields, work, gathered, weights_hi, weights_lo, blocks, planes0, planes1, planes2, smooth_sum,
      damp, source, peers, row_of, send_sems, recv_sems, plane_send, plane_recv, slot, links,
-     coords, taps, obs_ref, est_ref, load_sems) = scratch[2 * n :]
+     coords, taps, obs_ref, est_ref, load_sems, partly) = scratch[2 * n :]
     planes = (planes0, planes1, planes2)
     ssem = {name: send_sems.at[k] for k, name in enumerate(NAMES)}
     rsem = {name: recv_sems.at[k] for k, name in enumerate(NAMES)}
@@ -140,7 +141,7 @@
     lane = lax.broadcasted_iota(jnp.int32, (8, 128), 1)
     in_y = lax.rem(lane, 16)
 
-    def make_weights(slot_at, axis, flipped):
+    def make_weights(slot_at, axis, flipped, keep=None):
         a = lax.broadcasted_iota(jnp.int32, (128, 128), 1)
         b = lax.broadcasted_iota(jnp.int32, (128, 128), 0)
         for side in range(3):
@@ -161,11 +162,25 @@
                 return jnp.where(tap == t, taps[axis, t], total)
 
             block = lax.fori_loop(0, TAPS, pick, jnp.zeros((128, 128), f32))
-            high = block.astype(bf16)
-            low = (block - high.astype(f32)).astype(bf16)
-            cols = pl.ds(128 * side, 128)
-            weights_hi[slot_at, :, cols] = high
-            weights_lo[slot_at, :, cols] = low
+            if keep is not None:
+                blocks[keep, side] = block
+            if slot_at is not None:
+                hold_weights(slot_at, side, block)
+
+    def hold_weights(slot_at, at, block):
+        high = block.astype(bf16)
+        weights_hi[slot_at, :, 128 * at : 128 * at + 128] = high
+        weights_lo[slot_at, :, 128 * at : 128 * at + 128] = (block - high.astype(f32)).astype(bf16)
+
+    def both_x_passes(slot_at):
+        def through(back, forth):
+            return jnp.dot(blocks[1, back], blocks[0, forth], precision=lax.Precision.HIGHEST,
+                           preferred_element_type=f32)
+
+        hold_weights(slot_at, 0, through(1, 0) + through(0, 1))
+        hold_weights(slot_at, 1, through(1, 1))
+        hold_weights(slot_at, 2, through(1, 2) + through(2, 1))
+        hold_weights(slot_at, 3, through(0, 2) + through(2, 0))
 
     make_weights(0, 0, False)
     make_weights(1, 1, False)
@@ -178,8 +193,8 @@
 
         lax.fori_loop(0, 4, step, 0)
 
-    def gather(ref, axis):
-        def body(b):
+    def gather(ref, axis, ends=False):
+        for b in range(NB):
             own = ref[b]
             lower = ref[peers[b, 2 * axis]]
             upper = ref[peers[b, 2 * axis + 1]]
@@ -189,8 +204,11 @@
             gathered[b, :, 0:128] = lower
             gathered[b, :, 128:256] = own
             gathered[b, :, 256:384] = upper
-
-        bricks_loop(body)
+            if ends:
+                has_lower = jnp.where(peers[b, 4] < NB, 1.0, 0.0)
+                has_upper = jnp.where(peers[b, 5] < NB, 1.0, 0.0)
+                inner = jnp.where(lane >= 128 - REACH, own * has_upper, 0.0)
+                gathered[b, :, 384:512] = jnp.where(lane < REACH, own * has_lower, inner)
 
     def split(values):
         high = values.astype(bf16)
@@ -198,36 +216,36 @@
 
     NT = (((1,), (1,)), ((), ()))
 
+    def operands(ref, axis, which, ends):
+        gather(ref, axis, ends)
+        depth = 512 if ends else 384
+        high, low = split(gathered[:, :, 0:depth].reshape(256, depth))
+        return high, low, weights_hi[which, :, 0:depth], weights_lo[which, :, 0:depth]
+
+    def dot(a, b):
+        return lax.dot_general(a, b, NT, preferred_element_type=f32)
+
     def apply(ref, axis, which):
-        gather(ref, axis)
-        high, low = split(gathered[...].reshape(256, 384))
-        w_high, w_low = weights_hi[which], weights_lo[which]
-        return (
-            lax.dot_general(high, w_high, NT, preferred_element_type=f32)
-            + lax.dot_general(low, w_high, NT, preferred_element_type=f32)
-            + lax.dot_general(high, w_low, NT, preferred_element_type=f32)
-        )
-
-    def apply_turned(ref, axis, which):
-        gather(ref, axis)
-        high, low = split(gathered[...].reshape(256, 384))
-        w_high, w_low = weights_hi[which], weights_lo[which]
-        return (
-            lax.dot_general(w_high, high, NT, preferred_element_type=f32)
-            + lax.dot_general(w_high, low, NT, preferred_element_type=f32)
-            + lax.dot_general(w_low, high, NT, preferred_element_type=f32)
-        )
+        high, low, w_high, w_low = operands(ref, axis, which, False)
+        return dot(high, w_high) + dot(low, w_high) + dot(high, w_low)
+
+    def apply_turned(ref, axis, which, ends=False):
+        high, low, w_high, w_low = operands(ref, axis, which, ends)
+        return dot(w_high, high) + dot(w_high, low) + dot(w_low, high)
 
     def post(name, turned):
         rows = EXCHANGES[name][1]
         for h in range(2):
             send[name][pl.ds(h, 128, stride=rows), :] = turned[:, 128 * h : 128 * h + 128]
 
-    def unpack(name, ref):
+    def unpack(name, ref, scale=None):
         rows = EXCHANGES[name][1]
         for h in range(2):
             block = recv[name][pl.ds(h, 128, stride=rows), :].T
-            ref[16 * h : 16 * h + 16] = block.reshape(16, 8, 128)
+            block = block.reshape(16, 8, 128)
+            if scale is not None:
+                block = block * scale[16 * h : 16 * h + 16]
+            ref[16 * h : 16 * h + 16] = block
 
     def plane_copies(op):
         copies = []
@@ -273,7 +291,7 @@
             total = zero
             for before, beyond, low in sides:
                 total = total + penalty(own - before) * low - penalty(beyond - own)
-            smooth_sum[b] = WEIGHT * total
+            smooth_sum[op, b] = WEIGHT * total
 
         bricks_loop(body)
 
@@ -283,25 +301,23 @@
             total = zero
             for before, beyond, low in sides:
                 total = total + (own - before) * low - (beyond - own)
-            smooth_sum[b] = WEIGHT * total
+            smooth_sum[op, b] = WEIGHT * total
 
         bricks_loop(body)
 
-    def operate(op, out, to_zy, to_x, first, before_x=None, meanwhile=None):
+    def operate(op, to_zy, to_x, first, before_x=None, meanwhile=None):
         planes_moving = plane_copies(op)
-        for copy in planes_moving:
-            copy.start()
         work[0:NB] = apply(fields.at[op], 0, 0).reshape(NB, 8, 128)
         post(to_zy, apply_turned(work, 1, 1))
         start(to_zy)
+        for copy in planes_moving:
+            copy.start()
         if before_x is not None:
             before_x()
         arrive(to_zy)
-        unpack(to_zy, work)
-        blurred = apply(work, 2, 2).reshape(NB, 8, 128)
-        weighted = damp[...] * damp[...] * blurred
-        work[0:NB] = source[...] - weighted if first else weighted
-        post(to_x, apply_turned(work, 2, 3))
+        unpack(to_zy, work, damp)
+        turned = apply_turned(work, 2, 2, ends=True)
+        post(to_x, source[...] - turned if first else turned)
         start(to_x)
         for copy in planes_moving:
             copy.wait()
@@ -314,14 +330,15 @@
         arrive(to_x)
         unpack(to_x, work)
         work[0:NB] = apply(work, 1, 4).reshape(NB, 8, 128)
-        return apply(work, 0, 5).reshape(NB, 8, 128) + smooth_sum[...]
+        return apply(work, 0, 5).reshape(NB, 8, 128) + smooth_sum[op]
 
     arrive("est")
     fields[0, 0:NB] = recv["est"][...].reshape(NB, 8, 128)
 
     def prepare():
-        make_weights(2, 2, False)
-        make_weights(3, 2, True)
+        make_weights(None, 2, False, keep=0)
+        make_weights(3, 2, True, keep=1)
+        both_x_passes(2)
 
         def body(b):
             depth = coords[0, slot[b]] * 64 + 8 * sub + me // 16
@@ -329,19 +346,21 @@
 
         bricks_loop(body)
         arrive("obs")
-        source[...] = damp[...] * recv["obs"][...].reshape(NB, 8, 128)
+        work[0:NB] = damp[...] * recv["obs"][...].reshape(NB, 8, 128)
+        source[...] = apply_turned(work, 2, 3)
+        damp[...] = damp[...] * damp[...]
 
     def prepare_adjoint():
         make_weights(4, 1, True)
         make_weights(5, 0, True)
 
-    fields[1, 0:NB] = operate(0, 1, "t1", "t2", True, before_x=prepare, meanwhile=prepare_adjoint)
+    fields[1, 0:NB] = operate(0, "t1", "t2", True, before_x=prepare, meanwhile=prepare_adjoint)
 
     def send_r0():
         send["b0"][...] = fields[1, 0:NB].reshape(256, 128)
         start("b0")
 
-    fields[2, 0:NB] = operate(1, 2, "t3", "t4", False, before_x=send_r0)
+    fields[2, 0:NB] = operate(1, "t3", "t4", False, before_x=send_r0)
 
     low_half = lax.broadcasted_iota(jnp.int32, (1, 128), 1) < 64
 
@@ -354,58 +373,66 @@
 
     def send_w1():
         r0, w1 = fields[1, 0:NB].reshape(256, 128), fields[2, 0:NB].reshape(256, 128)
-        send["sums"][...] = jnp.broadcast_to(two_sums(r0 * r0, r0 * w1), (128, 128))
-        start("sums")
+        send["sums1"][...] = jnp.broadcast_to(two_sums(r0 * r0, r0 * w1), (128, 128))
+        start("sums1")
         send["b1"][...] = w1
         start("b1")
 
-    w2 = operate(2, None, "t5", "t6", False, before_x=send_w1).reshape(256, 128)
-
     def total_of(rows):
         return jnp.sum(rows, keepdims=True)
 
-    low = lax.broadcasted_iota(jnp.int32, (128, 128), 1) < 64
-    arrive("sums")
-    rr = total_of(jnp.where(low, recv["sums"][...], 0.0))
-    r0w1 = total_of(jnp.where(low, 0.0, recv["sums"][...]))
-    step1 = rr / r0w1
-
-    work[0:NB] = w2.reshape(NB, 8, 128)
-    r0, w1 = fields[1, 0:NB].reshape(256, 128), fields[2, 0:NB].reshape(256, 128)
-    r1 = r0 - step1 * w1
-    ar1 = w1 - step1 * w2
-    first_pair = two_sums(r1 * r1, r1 * ar1)
-    second_pair = two_sums(r1 * w1, r0 * ar1)
-    quarter = lax.rem(lax.broadcasted_iota(jnp.int32, (1, 128), 1), 64) < 32
-    first_pair = first_pair + pltpu.roll(first_pair, 96, 1)
-    second_pair = second_pair + pltpu.roll(second_pair, 32, 1)
-    sums = jnp.where(quarter, first_pair, second_pair)
-    w2_rows = w2.reshape(128, 2, 128)
-    for h in range(2):
-        send["t7"][pl.ds(h, 128, stride=4), :] = w2_rows[:, h, :]
-    send["t7"][pl.ds(2, 128, stride=4), :] = jnp.broadcast_to(sums, (128, 128))
+    lane_of = lax.broadcasted_iota(jnp.int32, (128, 128), 1)
+
+    def first_step():
+        arrive("sums1")
+        rr = total_of(jnp.where(lane_of < 64, recv["sums1"][...], 0.0))
+        r0w1 = total_of(jnp.where(lane_of < 64, 0.0, recv["sums1"][...]))
+        return rr, r0w1, rr / r0w1
+
+    def send_sums():
+        rr, r0w1, step1 = first_step()
+        r0, w1 = fields[1, 0:NB].reshape(256, 128), fields[2, 0:NB].reshape(256, 128)
+        r1 = r0 - step1 * w1
+        smooth1 = (smooth_sum[1] - step1 * smooth_sum[2]).reshape(256, 128)
+        blurred = recv["t3"][...] - step1 * recv["t5"][...]
+        passed = send["t4"][...] - step1 * send["t6"][...]
+        first_pair = two_sums(r1 * r1, r1 * smooth1 + blurred * passed)
+        second = jnp.sum(r1 * w1, axis=0, keepdims=True)
+        for shift in (64, 32):
+            second = second + pltpu.roll(second, shift, 1)
+        first_pair = first_pair + pltpu.roll(first_pair, 96, 1)
+        quarter = lax.rem(lax.broadcasted_iota(jnp.int32, (1, 128), 1), 64) < 32
+        send["sums2"][...] = jnp.broadcast_to(jnp.where(quarter, first_pair, second), (128, 128))
+        start("sums2")
+        steps.extend((rr, r0w1, step1))
+
+    steps = []
+    work_out = operate(2, "t5", "t6", False, before_x=send_w1, meanwhile=send_sums)
+    send["t7"][...] = work_out.reshape(256, 128)
     start("t7")
+    rr, r0w1, step1 = steps
     arrive("b0")
     arrive("b1")
-    arrive("t7")
-    sums = recv["t7"][pl.ds(2, 128, stride=4), :]
-    lane_of = lax.broadcasted_iota(jnp.int32, (128, 128), 1)
-    own = lax.rem(lane_of, 64) < 32
-    rr1 = total_of(jnp.where(own & low, sums, 0.0))
-    r1ar1 = total_of(jnp.where(own & (lane_of >= 64), sums, 0.0))
-    cross = total_of(jnp.where(own, 0.0, sums))
+    arrive("sums2")
+    sums = recv["sums2"][...]
+    inner = lax.rem(lane_of, 64) < 32
+    rr1 = total_of(jnp.where(inner & (lane_of < 64), sums, 0.0))
+    r1ar1 = total_of(jnp.where(inner & (lane_of >= 64), sums, 0.0))
+    r1w1 = total_of(jnp.where(lane_of < 64, jnp.where(inner, 0.0, sums), 0.0))
     ratio = rr1 / rr
-    step2 = rr1 / (r1ar1 + ratio * cross + ratio * ratio * r0w1)
+    step2 = rr1 / (r1ar1 + 2.0 * ratio * r1w1 + ratio * ratio * r0w1)
     for h in range(2):
         b0 = recv["b0"][pl.ds(h, 128, stride=2), :].T
         b1 = recv["b1"][pl.ds(h, 128, stride=2), :].T
-        b2 = recv["t7"][pl.ds(h, 128, stride=4), :].T
         r = b0 - step1 * b1
-        ar = b1 - step1 * b2
         est = est_ref[0, 8 * h : 8 * h + 8].reshape(128, 128)
         sol = est + step1 * b0 + step2 * (r + ratio * b0)
-        res = r - step2 * (ar + ratio * b1)
         sol_ref[0, 8 * h : 8 * h + 8] = sol.reshape(8, 16, 128)
+        partly[128 * h : 128 * h + 128] = r - step2 * (b1 + ratio * b1)
+    arrive("t7")
+    for h in range(2):
+        b2 = recv["t7"][pl.ds(h, 128, stride=2), :].T
+        res = partly[128 * h : 128 * h + 128] + step2 * step1 * b2
         res_ref[0, 8 * h : 8 * h + 8] = res.reshape(8, 16, 128)
 
     for name in NAMES:
@@ -427,13 +454,14 @@
         scratch_shapes=buffers + buffers + [
             pltpu.VMEM((3, NB + 1, 8, 128), f32),
             pltpu.VMEM((NB + 1, 8, 128), f32),
-            pltpu.VMEM((NB, 8, 384), f32),
-            pltpu.VMEM((6, 128, 384), bf16),
-            pltpu.VMEM((6, 128, 384), bf16),
+            pltpu.VMEM((NB, 8, 512), f32),
+            pltpu.VMEM((6, 128, 512), bf16),
+            pltpu.VMEM((6, 128, 512), bf16),
+            pltpu.VMEM((2, 3, 128, 128), f32),
             *[pltpu.VMEM((2, NB + 1, 8, 128), f32)] * 3,
+            pltpu.VMEM((3, NB, 8, 128), f32),
             pltpu.VMEM((NB, 8, 128), f32),
-            pltpu.VMEM((NB, 8, 128), f32),
-            pltpu.VMEM((NB, 8, 128), f32),
+            pltpu.VMEM((128, 256), f32),
             pltpu.SMEM((NB, 6), jnp.int32),
             pltpu.SMEM((NB,), jnp.int32),
             pltpu.SemaphoreType.DMA((count,)),
@@ -447,6 +475,7 @@
             pltpu.VMEM(observed.shape, f32),
             pltpu.VMEM(estimate.shape, f32),
             pltpu.SemaphoreType.DMA((6,)),
+            pltpu.VMEM((256, 128), f32),
         ],
         compiler_params=pltpu.CompilerParams(collective_id=0, has_side_effects=True),
         name="splitting_step",

time: 77.9 us -> 71.4 us (0.917)
  Pallas kernels: 74.9 us -> 68.4 us
    pallas_call x1, Pallas kernels: 74.9 us -> 68.4 us  [shards(): pl.pallas_call(kernel, out_shape=(shape, shape), in_specs=[place] * 6, ou...]
where the time goes in v3:
time: 71.4 us; the launch traced here: 71.3 us
  Pallas kernels  68.4 us (96%)
  local copies, waits for them, and re-layouts  2.26 us (3%)
    pallas_call x1, Pallas kernels, shards(): pl.pallas_call(kernel, out_shape=(shape, shape), in_specs=[place] * 6, ou...  68.4 us
    unnamed x4, local copies, waits for them, and re-layouts  2.26 us

profile of v3, /device:TPU:1, one launch (start us, length us, event | category | flops | bytes accessed | tf_op | source)
XLA Modules:
  0.0 71.3 jit_solution(11201988982212160750)
XLA Ops:
  0.6 68.4 %splitting_step.1 = (f32[1,16,16,128]{3,2,1,0:T(8,128)}, f32[1,16,16,128]{3,2,1,0:T(8,128)}) custom-call(s32[32]{0:T(128)} %slot_in.1, s32[6,32]{1,0:T(8,128)} %bitcast.2, s32[3,32]{1,0:T(4,128)} %bitcast.3, f32[3,15]{1,0:T(4,128)} %taps_in.1, f32[1,16,16,128]{3,2,1,0:T(8,128)} %obs_in.1, f32[1,16,16,128]{3,2,1,0:T(8,128)} %est_in.1), custom_call_target="tpu_custom_call" | custom-call | tf_op jit(solution)/shard_map/splitting_step/pallas_call | solution.py:449
  69.0 0.0 copy-start
  69.0 1.6 %copy.10 = f32[1,16,16,128]{3,2,1,0:T(8,128)} copy(f32[1,16,16,128]{3,2,1,0:T(8,128)} %get-tuple-element.4) | data formatting | bytes 262144
  70.6 0.0 copy-done
  70.6 0.7 copy.11
Async XLA Ops:
  69.0 1.6 %copy-start = (f32[1,16,16,128]{3,2,1,0:T(8,128)S(1)}, f32[1,16,16,128]{3,2,1,0:T(8,128)}, u32[]{:S(2)}) copy-start(f32[1,16,16,128]{3,2,1,0:T(8,128)} %get-tuple-element.5) | copy-start | bytes 393220

commit v4 on v3

--- a/solution.py
+++ b/solution.py
@@ -28,7 +28,7 @@
     n = len(NAMES)
     send = dict(zip(NAMES, scratch[:n]))
     recv = dict(zip(NAMES, scratch[n : 2 * n]))
-    (fields, work, gathered, weights_hi, weights_lo, blocks, planes0, planes1, planes2, smooth_sum,
+    (fields, work, gathered, weights, turned_weights, blocks, planes0, planes1, planes2, smooth_sum,
      damp, source, peers, row_of, send_sems, recv_sems, plane_send, plane_recv, slot, links,
      coords, taps, obs_ref, est_ref, load_sems, partly) = scratch[2 * n :]
     planes = (planes0, planes1, planes2)
@@ -141,9 +141,9 @@
     lane = lax.broadcasted_iota(jnp.int32, (8, 128), 1)
     in_y = lax.rem(lane, 16)
 
-    def make_weights(slot_at, axis, flipped, keep=None):
-        a = lax.broadcasted_iota(jnp.int32, (128, 128), 1)
-        b = lax.broadcasted_iota(jnp.int32, (128, 128), 0)
+    def make_weights(slot_at, axis, flipped, turned=False, keep=None):
+        a = lax.broadcasted_iota(jnp.int32, (128, 128), 1 if turned else 0)
+        b = lax.broadcasted_iota(jnp.int32, (128, 128), 0 if turned else 1)
         for side in range(3):
             if axis == 0:
                 tap = 8 * (side - 1) + a // 16 - b // 16 + REACH
@@ -164,26 +164,32 @@
             block = lax.fori_loop(0, TAPS, pick, jnp.zeros((128, 128), f32))
             if keep is not None:
                 blocks[keep, side] = block
-            if slot_at is not None:
-                hold_weights(slot_at, side, block)
-
-    def hold_weights(slot_at, at, block):
+            if turned and slot_at is not None:
+                hold_turned(slot_at, side, block)
+            elif slot_at is not None:
+                high = block.astype(bf16)
+                rows = pl.ds(128 * side, 128)
+                weights[slot_at, rows, 0:128] = high
+                weights[slot_at, rows, 128:256] = (block - high.astype(f32)).astype(bf16)
+
+    def hold_turned(slot_at, at, block):
         high = block.astype(bf16)
-        weights_hi[slot_at, :, 128 * at : 128 * at + 128] = high
-        weights_lo[slot_at, :, 128 * at : 128 * at + 128] = (block - high.astype(f32)).astype(bf16)
+        cols = pl.ds(128 * at, 128)
+        turned_weights[slot_at, 0:128, cols] = high
+        turned_weights[slot_at, 128:256, cols] = (block - high.astype(f32)).astype(bf16)
 
     def both_x_passes(slot_at):
         def through(back, forth):
             return jnp.dot(blocks[1, back], blocks[0, forth], precision=lax.Precision.HIGHEST,
                            preferred_element_type=f32)
 
-        hold_weights(slot_at, 0, through(1, 0) + through(0, 1))
-        hold_weights(slot_at, 1, through(1, 1))
-        hold_weights(slot_at, 2, through(1, 2) + through(2, 1))
-        hold_weights(slot_at, 3, through(0, 2) + through(2, 0))
+        hold_turned(slot_at, 0, through(1, 0) + through(0, 1))
+        hold_turned(slot_at, 1, through(1, 1))
+        hold_turned(slot_at, 2, through(1, 2) + through(2, 1))
+        hold_turned(slot_at, 3, through(0, 2) + through(2, 0))
 
     make_weights(0, 0, False)
-    make_weights(1, 1, False)
+    make_weights(0, 1, False, turned=True)
 
     def bricks_loop(body):
         def step(g, carry):
@@ -214,24 +220,25 @@
         high = values.astype(bf16)
         return high, (values - high.astype(f32)).astype(bf16)
 
-    NT = (((1,), (1,)), ((), ()))
-
-    def operands(ref, axis, which, ends):
+    def operands(ref, axis, ends):
         gather(ref, axis, ends)
         depth = 512 if ends else 384
-        high, low = split(gathered[:, :, 0:depth].reshape(256, depth))
-        return high, low, weights_hi[which, :, 0:depth], weights_lo[which, :, 0:depth]
-
-    def dot(a, b):
-        return lax.dot_general(a, b, NT, preferred_element_type=f32)
+        return depth, *split(gathered[:, :, 0:depth].reshape(256, depth))
+
+    def dot(a, b, contract):
+        return lax.dot_general(a, b, (contract, ((), ())), preferred_element_type=f32)
 
     def apply(ref, axis, which):
-        high, low, w_high, w_low = operands(ref, axis, which, False)
-        return dot(high, w_high) + dot(low, w_high) + dot(high, w_low)
+        _, high, low = operands(ref, axis, False)
+        both = dot(high, weights[which], ((1,), (0,)))
+        rest = dot(low, weights[which, :, 0:128], ((1,), (0,)))
+        return both[:, 0:128] + both[:, 128:256] + rest
 
     def apply_turned(ref, axis, which, ends=False):
-        high, low, w_high, w_low = operands(ref, axis, which, ends)
-        return dot(w_high, high) + dot(w_high, low) + dot(w_low, high)
+        depth, high, low = operands(ref, axis, ends)
+        both = dot(turned_weights[which, :, 0:depth], high, ((1,), (1,)))
+        rest = dot(turned_weights[which, 0:128, 0:depth], low, ((1,), (1,)))
+        return both[0:128] + both[128:256] + rest
 
     def post(name, turned):
         rows = EXCHANGES[name][1]
@@ -308,7 +315,7 @@
     def operate(op, to_zy, to_x, first, before_x=None, meanwhile=None):
         planes_moving = plane_copies(op)
         work[0:NB] = apply(fields.at[op], 0, 0).reshape(NB, 8, 128)
-        post(to_zy, apply_turned(work, 1, 1))
+        post(to_zy, apply_turned(work, 1, 0))
         start(to_zy)
         for copy in planes_moving:
             copy.start()
@@ -316,7 +323,7 @@
             before_x()
         arrive(to_zy)
         unpack(to_zy, work, damp)
-        turned = apply_turned(work, 2, 2, ends=True)
+        turned = apply_turned(work, 2, 1, ends=True)
         post(to_x, source[...] - turned if first else turned)
         start(to_x)
         for copy in planes_moving:
@@ -329,16 +336,16 @@
             meanwhile()
         arrive(to_x)
         unpack(to_x, work)
-        work[0:NB] = apply(work, 1, 4).reshape(NB, 8, 128)
-        return apply(work, 0, 5).reshape(NB, 8, 128) + smooth_sum[op]
+        work[0:NB] = apply(work, 1, 1).reshape(NB, 8, 128)
+        return apply(work, 0, 2).reshape(NB, 8, 128) + smooth_sum[op]
 
     arrive("est")
     fields[0, 0:NB] = recv["est"][...].reshape(NB, 8, 128)
 
     def prepare():
-        make_weights(None, 2, False, keep=0)
-        make_weights(3, 2, True, keep=1)
-        both_x_passes(2)
+        make_weights(None, 2, False, turned=True, keep=0)
+        make_weights(2, 2, True, turned=True, keep=1)
+        both_x_passes(1)
 
         def body(b):
             depth = coords[0, slot[b]] * 64 + 8 * sub + me // 16
@@ -347,12 +354,12 @@
         bricks_loop(body)
         arrive("obs")
         work[0:NB] = damp[...] * recv["obs"][...].reshape(NB, 8, 128)
-        source[...] = apply_turned(work, 2, 3)
+        source[...] = apply_turned(work, 2, 2)
         damp[...] = damp[...] * damp[...]
 
     def prepare_adjoint():
-        make_weights(4, 1, True)
-        make_weights(5, 0, True)
+        make_weights(1, 1, True)
+        make_weights(2, 0, True)
 
     fields[1, 0:NB] = operate(0, "t1", "t2", True, before_x=prepare, meanwhile=prepare_adjoint)
 
@@ -455,8 +462,8 @@
             pltpu.VMEM((3, NB + 1, 8, 128), f32),
             pltpu.VMEM((NB + 1, 8, 128), f32),
             pltpu.VMEM((NB, 8, 512), f32),
-            pltpu.VMEM((6, 128, 512), bf16),
-            pltpu.VMEM((6, 128, 512), bf16),
+            pltpu.VMEM((3, 384, 256), bf16),
+            pltpu.VMEM((3, 256, 512), bf16),
             pltpu.VMEM((2, 3, 128, 128), f32),
             *[pltpu.VMEM((2, NB + 1, 8, 128), f32)] * 3,
             pltpu.VMEM((3, NB, 8, 128), f32),

time: 71.4 us -> 70.3 us (0.985)
  Pallas kernels: 68.4 us -> 67.3 us
    pallas_call x1, Pallas kernels: 68.4 us -> 67.3 us  [shards(): pl.pallas_call(kernel, out_shape=(shape, shape), in_specs=[place] * 6, ou...]
where the time goes in v4:
time: 70.3 us; the launch traced here: 70.2 us
  Pallas kernels  67.3 us (96%)
  local copies, waits for them, and re-layouts  2.26 us (3%)
    pallas_call x1, Pallas kernels, shards(): pl.pallas_call(kernel, out_shape=(shape, shape), in_specs=[place] * 6, ou...  67.3 us
    unnamed x4, local copies, waits for them, and re-layouts  2.26 us

profile of v4, /device:TPU:1, one launch (start us, length us, event | category | flops | bytes accessed | tf_op | source)
XLA Modules:
  0.0 70.2 jit_solution(16807869363285594427)
XLA Ops:
  0.6 67.3 %splitting_step.1 = (f32[1,16,16,128]{3,2,1,0:T(8,128)}, f32[1,16,16,128]{3,2,1,0:T(8,128)}) custom-call(s32[32]{0:T(128)} %slot_in.1, s32[6,32]{1,0:T(8,128)} %bitcast.2, s32[3,32]{1,0:T(4,128)} %bitcast.3, f32[3,15]{1,0:T(4,128)} %taps_in.1, f32[1,16,16,128]{3,2,1,0:T(8,128)} %obs_in.1, f32[1,16,16,128]{3,2,1,0:T(8,128)} %est_in.1), custom_call_target="tpu_custom_call" | custom-call | tf_op jit(solution)/shard_map/splitting_step/pallas_call | solution.py:456
  67.9 0.0 copy-start
  67.9 1.6 %copy.10 = f32[1,16,16,128]{3,2,1,0:T(8,128)} copy(f32[1,16,16,128]{3,2,1,0:T(8,128)} %get-tuple-element.4) | data formatting | bytes 262144
  69.5 0.0 copy-done
  69.5 0.7 copy.11
Async XLA Ops:
  67.9 1.6 %copy-start = (f32[1,16,16,128]{3,2,1,0:T(8,128)S(1)}, f32[1,16,16,128]{3,2,1,0:T(8,128)}, u32[]{:S(2)}) copy-start(f32[1,16,16,128]{3,2,1,0:T(8,128)} %get-tuple-element.5) | copy-start | bytes 393220

commit v5 on v4

--- a/solution.py
+++ b/solution.py
@@ -24,13 +24,13 @@
 NAMES = list(EXCHANGES)
 
 
-def kernel(slot_in, links_in, coords_in, taps_in, obs_in, est_in, sol_ref, res_ref, *scratch):
+def kernel(slot_in, links_in, coords_in, taps_in, obs_in, est_in, sol_out, res_out, *scratch):
     n = len(NAMES)
     send = dict(zip(NAMES, scratch[:n]))
     recv = dict(zip(NAMES, scratch[n : 2 * n]))
     (fields, work, gathered, weights, turned_weights, blocks, planes0, planes1, planes2, smooth_sum,
      damp, source, peers, row_of, send_sems, recv_sems, plane_send, plane_recv, slot, links,
-     coords, taps, obs_ref, est_ref, load_sems, partly) = scratch[2 * n :]
+     coords, taps, obs_ref, est_ref, load_sems, partly, sol_ref, res_ref, store_sems) = scratch[2 * n :]
     planes = (planes0, planes1, planes2)
     ssem = {name: send_sems.at[k] for k, name in enumerate(NAMES)}
     rsem = {name: recv_sems.at[k] for k, name in enumerate(NAMES)}
@@ -436,28 +436,51 @@
         sol = est + step1 * b0 + step2 * (r + ratio * b0)
         sol_ref[0, 8 * h : 8 * h + 8] = sol.reshape(8, 16, 128)
         partly[128 * h : 128 * h + 128] = r - step2 * (b1 + ratio * b1)
+    stores = [pltpu.make_async_copy(sol_ref, sol_out, store_sems.at[0])]
+    stores[0].start()
     arrive("t7")
     for h in range(2):
         b2 = recv["t7"][pl.ds(h, 128, stride=2), :].T
         res = partly[128 * h : 128 * h + 128] + step2 * step1 * b2
         res_ref[0, 8 * h : 8 * h + 8] = res.reshape(8, 16, 128)
-
+        half = pl.ds(8 * h, 8)
+        stores.append(
+            pltpu.make_async_copy(res_ref.at[:, half], res_out.at[:, half], store_sems.at[1 + h]))
+        stores[-1].start()
+
+    for store in stores:
+        store.wait()
     for name in NAMES:
         sent = send[name].at[pl.ds(0, (ND - 1) * EXCHANGES[name][0])]
         pltpu.make_async_copy(sent, sent, ssem[name]).wait()
 
 
+def hand_over(sol_in, res_in, sol_out, res_out, held, load_sems, store_sems):
+    loads, stores = [], []
+    for k, (src, dst) in enumerate(((sol_in, sol_out), (res_in, res_out))):
+        for h in range(2):
+            half = pl.ds(8 * h, 8)
+            here = held.at[k, :, half]
+            loads.append(pltpu.make_async_copy(src.at[:, half], here, load_sems.at[2 * k + h]))
+            stores.append(pltpu.make_async_copy(here, dst.at[:, half], store_sems.at[2 * k + h]))
+            loads[-1].start()
+    for load, store in zip(loads, stores):
+        load.wait()
+        store.start()
+    for store in stores:
+        store.wait()
+
+
 def shards(observed, estimate, blur_taps, slot_brick, neighbours, coords):
     place = pl.BlockSpec(memory_space=pl.ANY)
-    vmem = pl.BlockSpec(memory_space=pltpu.VMEM)
     shape = jax.ShapeDtypeStruct(estimate.shape, f32)
     buffers = [pltpu.VMEM((ND * EXCHANGES[name][1], 128), f32) for name in NAMES]
     count = len(NAMES)
-    return pl.pallas_call(
+    found = pl.pallas_call(
         kernel,
         out_shape=(shape, shape),
         in_specs=[place] * 6,
-        out_specs=(vmem, vmem),
+        out_specs=(place, place),
         scratch_shapes=buffers + buffers + [
             pltpu.VMEM((3, NB + 1, 8, 128), f32),
             pltpu.VMEM((NB + 1, 8, 128), f32),
@@ -483,10 +506,25 @@
             pltpu.VMEM(estimate.shape, f32),
             pltpu.SemaphoreType.DMA((6,)),
             pltpu.VMEM((256, 128), f32),
+            pltpu.VMEM(estimate.shape, f32),
+            pltpu.VMEM(estimate.shape, f32),
+            pltpu.SemaphoreType.DMA((3,)),
         ],
         compiler_params=pltpu.CompilerParams(collective_id=0, has_side_effects=True),
         name="splitting_step",
     )(slot_brick, neighbours.T, coords.T, blur_taps, observed, estimate)
+    return pl.pallas_call(
+        hand_over,
+        out_shape=(shape, shape),
+        in_specs=[place] * 2,
+        out_specs=(place, place),
+        scratch_shapes=[
+            pltpu.VMEM((2, *estimate.shape), f32),
+            pltpu.SemaphoreType.DMA((4,)),
+            pltpu.SemaphoreType.DMA((4,)),
+        ],
+        name="hand_over",
+    )(*found)
 
 
 def solution(mesh):

time: 70.3 us -> 69.7 us (level)
  local copies, waits for them, and re-layouts: 2.26 us -> 0 us
  Pallas kernels: 67.3 us -> 68.8 us
    unnamed x4 -> x0, local copies, waits for them, and re-layouts: 2.26 us -> none
    pallas_call x0 -> x1, Pallas kernels: none -> 1.63 us  [shards(): pl.pallas_call(hand_over, out_shape=(shape, shape), in_specs=[place] * 2,...]
where the time goes in v5:
time: 69.7 us; the launch traced here: 69.5 us
  Pallas kernels  68.8 us (99%)
    pallas_call x1, Pallas kernels, shards(): pl.pallas_call(kernel, out_shape=(shape, shape), in_specs=[place] * 6, ou...  67.2 us
    pallas_call x1, Pallas kernels, shards(): pl.pallas_call(hand_over, out_shape=(shape, shape), in_specs=[place] * 2,...  1.63 us

profile of v5, /device:TPU:1, one launch (start us, length us, event | category | flops | bytes accessed | tf_op | source)
XLA Modules:
  0.0 69.5 jit_solution(3587891333451629109)
XLA Ops:
  0.6 67.2 %splitting_step.1 = (f32[1,16,16,128]{3,2,1,0:T(8,128)}, f32[1,16,16,128]{3,2,1,0:T(8,128)}) custom-call(s32[32]{0:T(128)} %slot_in.1, s32[6,32]{1,0:T(8,128)} %bitcast.2, s32[3,32]{1,0:T(4,128)} %bitcast.3, f32[3,15]{1,0:T(4,128)} %taps_in.1, f32[1,16,16,128]{3,2,1,0:T(8,128)} %obs_in.1, f32[1,16,16,128]{3,2,1,0:T(8,128)} %est_in.1), custom_call_target="tpu_custom_call" | custom-call | tf_op jit(solution)/shard_map/splitting_step/pallas_call | solution.py:479
  67.8 1.6 %hand_over.1 = (f32[1,16,16,128]{3,2,1,0:T(8,128)}, f32[1,16,16,128]{3,2,1,0:T(8,128)}) custom-call(f32[1,16,16,128]{3,2,1,0:T(8,128)} %get-tuple-element.4.sol_in, f32[1,16,16,128]{3,2,1,0:T(8,128)} %get-tuple-element.5.res_in), custom_call_target="tpu_custom_call" | custom-call | tf_op jit(solution)/shard_map/hand_over/pallas_call | solution.py:516
